TPU v7x, 32 devices: a whole 2x2x4 slice. The times are simulated.
32 devices in a mesh: slab: 4 (over x, core), kt: 8 (over z, y).
Axes of the slice: x: 2, y: 2, z: 4, core: 2. Of those that a mesh axis runs over, the one named last changes fastest.
Arguments:
- energies: float32 [4], replicated, may hold values from -0.5 to 0.1
- onsite: float32 [8, 4, 384], P('kt', 'slab'), may hold values from -3.5 to -2.5
- hamiltonian: bfloat16 [8, 4, 2, 384, 384], P('kt', 'slab'), may hold values from -0.109375 to 0.109375
- hopping: bfloat16 [8, 4, 2, 384, 384], P('kt', 'slab'), may hold values from -0.15625 to 0.15625
- contact: bfloat16 [8, 2, 384, 384], P('kt'), may hold values from -2 to 2
- previous: bfloat16 [8, 4, 4, 2, 2, 384, 384], P('kt', None, 'slab'), may hold values from -4 to 4
- neighbours: int32 [8, 2], P('kt'), may hold values from 0 to 7, as said below
- mode_index: int32 [8, 2], P('kt'), may hold values from 0 to 3
- mode_strength: float32 [4], replicated, may hold values from 0.25 to 1
Outputs:
- retarded: bfloat16 [8, 4, 4, 2, 384, 384], P('kt', None, 'slab')
- lesser: bfloat16 [8, 4, 4, 2, 384, 384], P('kt', None, 'slab')
Inputs may be any that keep to these rules, and one draw needn't show every extreme that they name: neighbours[k, 0] is k - 1 or k - 2 and neighbours[k, 1] is k + 1 or k + 2, modulo 8.
All inputs are finite; a program needn't handle non-finite values.
Results may differ from a plain program's by a relative error of at most 0.017.
Values may be sent and summed in bfloat16 or wider, within the bound.
A program may use at most 128 MiB of HBM per device.

v0:
```python
import jax
import jax.numpy as jnp
from jax import lax
from jax.sharding import PartitionSpec as P

broaden = 0.05
fermi_level = 0.0
thermal = 0.1


def from_behind(value, axis, by):
    peers = lax.axis_size(axis)
    return lax.ppermute(value, axis, [(i, (i + by) % peers) for i in range(peers)])


def as_sent(value):
    return jax.tree.map(lambda a: a.astype(jnp.bfloat16) if a.dtype == jnp.float32 else a, value)


def combine(pieces):
    real_part = pieces[..., 0, 0, :, :] - pieces[..., 1, 1, :, :]
    imaginary_part = pieces[..., 0, 1, :, :] + pieces[..., 1, 0, :, :]
    return jnp.stack([real_part, imaginary_part], axis=-3)


def complex_mul(first_op, second_op):
    return combine(
        jnp.einsum("pij,qjk->pqik", first_op, second_op, preferred_element_type=jnp.float32)
    )


def adjoint(matrix):
    return jnp.stack([matrix[0].T, -matrix[1].T])


def mul_adjoint(first_op, second_op):
    pieces = jnp.einsum(
        "...pij,qkj->...pqik", first_op, second_op, preferred_element_type=jnp.float32
    )
    real_part = pieces[..., 0, 0, :, :] + pieces[..., 1, 1, :, :]
    imaginary_part = pieces[..., 1, 0, :, :] - pieces[..., 0, 1, :, :]
    return jnp.stack([real_part, imaginary_part], axis=-3)


def slab_update(boundary, energy, levels, hamilton, coupling, phonon):
    moved_blocks = combine(
        jnp.einsum("pij,sqjk->spqik", coupling, boundary, preferred_element_type=jnp.float32)
    ).astype(jnp.bfloat16)
    self_both = mul_adjoint(moved_blocks, coupling)
    self_retarded = self_both[0]
    self_lesser = self_both[1]
    size = levels.shape[0]
    on_diagonal = lax.broadcasted_iota(jnp.int32, (size, size), 0) == lax.broadcasted_iota(
        jnp.int32, (size, size), 1
    )
    system_real = (
        jnp.where(on_diagonal, (energy - levels)[:, None], 0.0)
        - hamilton[0].astype(jnp.float32)
        - self_retarded[0]
        - phonon[0, 0]
    )
    system_imaginary = (
        jnp.where(on_diagonal, broaden, 0.0)
        - hamilton[1].astype(jnp.float32)
        - self_retarded[1]
        - phonon[0, 1]
    )
    diagonal_real = jnp.sum(jnp.where(on_diagonal, system_real, 0.0), axis=1)
    diagonal_imaginary = jnp.sum(jnp.where(on_diagonal, system_imaginary, 0.0), axis=1)
    modulus = diagonal_real * diagonal_real + diagonal_imaginary * diagonal_imaginary
    inverse_real = diagonal_real / modulus
    inverse_imaginary = -diagonal_imaginary / modulus
    scaled_real = (
        inverse_real[:, None] * system_real - inverse_imaginary[:, None] * system_imaginary
    )
    scaled_imaginary = (
        inverse_real[:, None] * system_imaginary + inverse_imaginary[:, None] * system_real
    )
    sandwich_real = (
        scaled_real * inverse_real[None, :] - scaled_imaginary * inverse_imaginary[None, :]
    )
    sandwich_imaginary = (
        scaled_real * inverse_imaginary[None, :] + scaled_imaginary * inverse_real[None, :]
    )
    first_guess = jnp.stack(
        [
            jnp.where(on_diagonal, 2.0 * inverse_real[:, None], 0.0) - sandwich_real,
            jnp.where(on_diagonal, 2.0 * inverse_imaginary[:, None], 0.0) - sandwich_imaginary,
        ]
    )
    first_rounded = first_guess.astype(jnp.bfloat16)
    system_rounded = jnp.stack([system_real, system_imaginary]).astype(jnp.bfloat16)
    product = complex_mul(system_rounded, first_rounded).astype(jnp.bfloat16)
    retarded = (2.0 * first_guess - complex_mul(first_rounded, product)).astype(jnp.bfloat16)
    source = (phonon[1] + self_lesser).astype(jnp.bfloat16)
    halfway = complex_mul(retarded, source).astype(jnp.bfloat16)
    lesser = mul_adjoint(halfway, retarded).astype(jnp.bfloat16)
    return (retarded, lesser)


def sweep_energy(boundary, energy, phonon, level_all, hamilton_all, coupling_all):
    slab_count = level_all.shape[0]
    retarded_list = [None] * slab_count
    lesser_list = [None] * slab_count
    for slab_num in reversed(range(slab_count)):
        ret_block, les_block = slab_update(
            boundary,
            energy,
            level_all[slab_num],
            hamilton_all[slab_num],
            coupling_all[slab_num],
            phonon[slab_num],
        )
        retarded_list[slab_num] = ret_block
        lesser_list[slab_num] = les_block
        boundary = jnp.stack([ret_block, les_block])
    return (jnp.stack(retarded_list), jnp.stack(lesser_list), boundary)


def cycle_phonon(blocks, neighbours, mode_index, mode_strength):
    nearest = [from_behind(blocks, "kt", offset) for offset in (1, -1)]
    farther = [from_behind(blocks, "kt", offset) for offset in (2, -2)]
    kpoint = lax.axis_index("kt")
    cycle_size = lax.axis_size("kt")
    neighbour_pair = neighbours[0]
    behind = jnp.where(neighbour_pair[0] == (kpoint - 1) % cycle_size, nearest[0], farther[0])
    forward = jnp.where(neighbour_pair[1] == (kpoint + 1) % cycle_size, nearest[1], farther[1])
    mode_table = jnp.arange(mode_strength.shape[0], dtype=jnp.int32)
    strength = jnp.sum(
        jnp.where(mode_index[0][:, None] == mode_table[None, :], mode_strength[None, :], 0.0),
        axis=1,
    )
    return (strength, behind, forward)


def weigh(strength, behind, forward):
    return strength[0] * behind.astype(jnp.float32) + strength[1] * forward.astype(jnp.float32)


def starting_blocks(contact, energy_list):
    contact_block = contact[0]
    contact_float = contact_block.astype(jnp.float32)
    skew_part = jnp.stack(
        [contact_float[0] - contact_float[0].T, contact_float[1] + contact_float[1].T]
    )
    occupation = 1.0 / (1.0 + jnp.exp((energy_list - fermi_level) / thermal))
    energy_count = energy_list.shape[0]
    contact_lesser = (-occupation[:, None, None, None] * skew_part).astype(jnp.bfloat16)
    return jnp.stack(
        [jnp.broadcast_to(contact_block, (energy_count,) + contact_block.shape), contact_lesser],
        axis=1,
    )


def body(
    energies, onsite, hamiltonian, hopping, contact, previous, neighbours, mode_index, mode_strength
):
    position = lax.axis_index("slab")
    half = previous.shape[5] // 2
    halves = [
        lax.all_to_all(
            previous[:, :, :, :, :, h * half : (h + 1) * half],
            "slab",
            split_axis=1,
            concat_axis=2,
            tiled=True,
        )
        for h in range(2)
    ]
    slab_total = halves[0].shape[2]
    slab_list = [None] * slab_total
    for slab_num in reversed(range(slab_total)):
        row_list = []
        for regrouped in halves:
            strength, behind, forward = cycle_phonon(
                regrouped[:, :, slab_num : slab_num + 1], neighbours, mode_index, mode_strength
            )
            row_list.append(weigh(strength, behind[0], forward[0]))
        slab_list[slab_num] = jnp.concatenate(row_list, axis=4)
    phonon_all = jnp.concatenate(slab_list, axis=1)
    level_whole = lax.all_gather(onsite, "slab", axis=1, tiled=True)
    hamilton_whole, coupling_whole = (
        lax.all_gather(hamiltonian, "slab", axis=1, tiled=True),
        lax.all_gather(hopping, "slab", axis=1, tiled=True),
    )
    local_count = phonon_all.shape[0]
    local_energies = lax.dynamic_slice_in_dim(energies, position * local_count, local_count, 0)
    initial = starting_blocks(contact, local_energies)

    def run_whole(boundary, energy, phonon):
        return sweep_energy(
            boundary, energy, phonon, level_whole[0], hamilton_whole[0], coupling_whole[0]
        )

    retarded_local, lesser_local, unused = jax.vmap(run_whole)(initial, local_energies, phonon_all)
    both_all = lax.all_to_all(
        as_sent(jnp.stack([retarded_local, lesser_local])[:, None]),
        "slab",
        split_axis=3,
        concat_axis=2,
        tiled=True,
    )
    return (both_all[0], both_all[1])


def solution(mesh):
    in_specs = (
        P(),
        P("kt", "slab", None),
        P("kt", "slab", None, None, None),
        P("kt", "slab", None, None, None),
        P("kt", None, None, None),
        P("kt", None, "slab", None, None, None, None),
        P("kt", None),
        P("kt", None),
        P(),
    )
    out_specs = (P("kt", None, "slab", None, None, None), P("kt", None, "slab", None, None, None))
    return jax.shard_map(body, mesh=mesh, in_specs=in_specs, out_specs=out_specs, check_vma=False)
```

profile of v0, /device:TPU:0, one launch (start us, length us, event | category | flops | bytes accessed | tf_op | source)
XLA Modules:
  0.0 550.2 jit_solution(13757800717214204489)
XLA Ops:
  7.2 5.2 fusion.324
  12.4 4.2 all-to-all-start.1
  17.4 40.4 %all-to-all-done.1 = bf16[1,4,1,2,2,192,384]{6,5,4,3,2,0,1:T(8,128)(2,1)S(1)} async-done(((bf16[1,4,1,2,2,192,384]{6,5,4,3,2,0,1:T(8,128)(2,1)}), bf16[1,4,1,2,2,192,384]{6,5,4,3,2,0,1:T(8,128)(2,1)S(1)}, u32[]{:S(2)}, u32[]{:S(2)}) %all-to-all-start.1) | async-done | bytes 2359328 | tf_op jit(solution)/shard_map/all_to_all | solution.py:161
  59.2 3.6 all-to-all-start
  62.9 2.9 fusion.327
  65.8 5.4 collective-permute-start.6
  73.2 18.1 %all-to-all-done = bf16[1,4,1,2,2,192,384]{6,5,4,3,2,0,1:T(8,128)(2,1)S(1)} async-done(((bf16[1,4,1,2,2,192,384]{6,5,4,3,2,0,1:T(8,128)(2,1)}), bf16[1,4,1,2,2,192,384]{6,5,4,3,2,0,1:T(8,128)(2,1)S(1)}, u32[]{:S(2)}, u32[]{:S(2)}) %all-to-all-start) | async-done | bytes 2359328 | tf_op jit(solution)/shard_map/all_to_all | solution.py:161
  92.8 5.4 collective-permute-start.2
  100.9 10.6 %collective-permute-done.5 = bf16[1,1,1,2,2,192,384]{6,5,4,3,2,1,0:T(8,128)(2,1)} collective-permute-done((bf16[1,1,1,2,2,192,384]{6,5,4,3,2,1,0:T(8,128)(2,1)}, bf16[1,1,1,2,2,192,384]{6,5,4,3,2,1,0:T(8,128)(2,1)}, u32[]{:S(2)}, u32[]{:S(2)}) %collective-permute-start.5) | collective-permute-done | bytes 589856 | tf_op jit(solution)/shard_map/ppermute | solution.py:13
  111.5 3.9 collective-permute-start.14
  115.4 7.8 %collective-permute-done.2 = bf16[1,1,1,2,2,192,384]{6,5,4,3,2,1,0:T(8,128)(2,1)S(1)} collective-permute-done((bf16[1,1,1,2,2,192,384]{6,5,4,3,2,1,0:T(8,128)(2,1)}, bf16[1,1,1,2,2,192,384]{6,5,4,3,2,1,0:T(8,128)(2,1)S(1)}, u32[]{:S(2)}, u32[]{:S(2)}) %collective-permute-start.2) | collective-permute-done | bytes 589856 | tf_op jit(solution)/shard_map/ppermute | solution.py:13
  123.7 12.5 %collective-permute-done.3 = bf16[1,1,1,2,2,192,384]{6,5,4,3,2,1,0:T(8,128)(2,1)S(1)} collective-permute-done((bf16[1,1,1,2,2,192,384]{6,5,4,3,2,1,0:T(8,128)(2,1)}, bf16[1,1,1,2,2,192,384]{6,5,4,3,2,1,0:T(8,128)(2,1)S(1)}, u32[]{:S(2)}, u32[]{:S(2)}) %collective-permute-start.3) | collective-permute-done | bytes 589856 | tf_op jit(solution)/shard_map/ppermute | solution.py:13
  138.9 10.5 %collective-permute-done.1 = bf16[1,1,1,2,2,192,384]{6,5,4,3,2,1,0:T(8,128)(2,1)S(1)} collective-permute-done((bf16[1,1,1,2,2,192,384]{6,5,4,3,2,1,0:T(8,128)(2,1)}, bf16[1,1,1,2,2,192,384]{6,5,4,3,2,1,0:T(8,128)(2,1)S(1)}, u32[]{:S(2)}, u32[]{:S(2)}) %collective-permute-start.1) | collective-permute-done | bytes 589856 | tf_op jit(solution)/shard_map/ppermute | solution.py:13
  149.4 3.8 collective-permute-start.10
  153.2 7.8 %collective-permute-done.14 = bf16[1,1,1,2,2,192,384]{6,5,4,3,2,1,0:T(8,128)(2,1)S(1)} collective-permute-done((bf16[1,1,1,2,2,192,384]{6,5,4,3,2,1,0:T(8,128)(2,1)S(1)}, bf16[1,1,1,2,2,192,384]{6,5,4,3,2,1,0:T(8,128)(2,1)S(1)}, u32[]{:S(2)}, u32[]{:S(2)}) %collective-permute-start.14) | collective-permute-done | bytes 589856 | tf_op jit(solution)/shard_map/ppermute | solution.py:13
  161.6 12.7 %collective-permute-done.15 = bf16[1,1,1,2,2,192,384]{6,5,4,3,2,1,0:T(8,128)(2,1)} collective-permute-done((bf16[1,1,1,2,2,192,384]{6,5,4,3,2,1,0:T(8,128)(2,1)S(1)}, bf16[1,1,1,2,2,192,384]{6,5,4,3,2,1,0:T(8,128)(2,1)}, u32[]{:S(2)}, u32[]{:S(2)}) %collective-permute-start.15) | collective-permute-done | bytes 589856 | tf_op jit(solution)/shard_map/ppermute | solution.py:13
  176.9 10.6 %collective-permute-done.13 = bf16[1,1,1,2,2,192,384]{6,5,4,3,2,1,0:T(8,128)(2,1)} collective-permute-done((bf16[1,1,1,2,2,192,384]{6,5,4,3,2,1,0:T(8,128)(2,1)S(1)}, bf16[1,1,1,2,2,192,384]{6,5,4,3,2,1,0:T(8,128)(2,1)}, u32[]{:S(2)}, u32[]{:S(2)}) %collective-permute-start.13) | collective-permute-done | bytes 589856 | tf_op jit(solution)/shard_map/ppermute | solution.py:13
  187.5 3.8 collective-permute-start.22
  196.7 5.2 all_gather.9
  202.7 9.5 %collective-permute-done.11 = bf16[1,1,1,2,2,192,384]{6,5,4,3,2,1,0:T(8,128)(2,1)} collective-permute-done((bf16[1,1,1,2,2,192,384]{6,5,4,3,2,1,0:T(8,128)(2,1)}, bf16[1,1,1,2,2,192,384]{6,5,4,3,2,1,0:T(8,128)(2,1)}, u32[]{:S(2)}, u32[]{:S(2)}) %collective-permute-start.11) | collective-permute-done | bytes 589856 | tf_op jit(solution)/shard_map/ppermute | solution.py:13
  214.9 10.6 %collective-permute-done.9 = bf16[1,1,1,2,2,192,384]{6,5,4,3,2,1,0:T(8,128)(2,1)} collective-permute-done((bf16[1,1,1,2,2,192,384]{6,5,4,3,2,1,0:T(8,128)(2,1)}, bf16[1,1,1,2,2,192,384]{6,5,4,3,2,1,0:T(8,128)(2,1)}, u32[]{:S(2)}, u32[]{:S(2)}) %collective-permute-start.9) | collective-permute-done | bytes 589856 | tf_op jit(solution)/shard_map/ppermute | solution.py:13
  225.5 3.7 collective-permute-start.18
  229.2 7.9 %collective-permute-done.22 = bf16[1,1,1,2,2,192,384]{6,5,4,3,2,1,0:T(8,128)(2,1)} collective-permute-done((bf16[1,1,1,2,2,192,384]{6,5,4,3,2,1,0:T(8,128)(2,1)}, bf16[1,1,1,2,2,192,384]{6,5,4,3,2,1,0:T(8,128)(2,1)}, u32[]{:S(2)}, u32[]{:S(2)}) %collective-permute-start.22) | collective-permute-done | bytes 589856 | tf_op jit(solution)/shard_map/ppermute | solution.py:13
  242.8 2.3 copy.242
  245.0 2.3 copy.243
  259.9 5.2 collective-permute-start.16
  265.1 3.3 collective-permute-start.30
  268.4 6.7 %collective-permute-done.18 = bf16[1,1,1,2,2,192,384]{6,5,4,3,2,1,0:T(8,128)(2,1)} collective-permute-done((bf16[1,1,1,2,2,192,384]{6,5,4,3,2,1,0:T(8,128)(2,1)}, bf16[1,1,1,2,2,192,384]{6,5,4,3,2,1,0:T(8,128)(2,1)}, u32[]{:S(2)}, u32[]{:S(2)}) %collective-permute-start.18) | collective-permute-done | bytes 589856 | tf_op jit(solution)/shard_map/ppermute | solution.py:13
  275.7 12.3 %collective-permute-done.19 = bf16[1,1,1,2,2,192,384]{6,5,4,3,2,1,0:T(8,128)(2,1)} collective-permute-done((bf16[1,1,1,2,2,192,384]{6,5,4,3,2,1,0:T(8,128)(2,1)}, bf16[1,1,1,2,2,192,384]{6,5,4,3,2,1,0:T(8,128)(2,1)}, u32[]{:S(2)}, u32[]{:S(2)}) %collective-permute-start.19) | collective-permute-done | bytes 589856 | tf_op jit(solution)/shard_map/ppermute | solution.py:13
  288.0 3.2 add_bitcast_fusion.6
  291.3 3.2 add_bitcast_fusion.7
  295.7 5.7 %collective-permute-done.17 = bf16[1,1,1,2,2,192,384]{6,5,4,3,2,1,0:T(8,128)(2,1)S(1)} collective-permute-done((bf16[1,1,1,2,2,192,384]{6,5,4,3,2,1,0:T(8,128)(2,1)}, bf16[1,1,1,2,2,192,384]{6,5,4,3,2,1,0:T(8,128)(2,1)S(1)}, u32[]{:S(2)}, u32[]{:S(2)}) %collective-permute-start.17) | collective-permute-done | bytes 589856 | tf_op jit(solution)/shard_map/ppermute | solution.py:13
  301.4 3.5 collective-permute-start.26
  304.9 8.2 %collective-permute-done.30 = bf16[1,1,1,2,2,192,384]{6,5,4,3,2,1,0:T(8,128)(2,1)S(1)} collective-permute-done((bf16[1,1,1,2,2,192,384]{6,5,4,3,2,1,0:T(8,128)(2,1)}, bf16[1,1,1,2,2,192,384]{6,5,4,3,2,1,0:T(8,128)(2,1)S(1)}, u32[]{:S(2)}, u32[]{:S(2)}) %collective-permute-start.30) | collective-permute-done | bytes 589856 | tf_op jit(solution)/shard_map/ppermute | solution.py:13
  313.7 12.1 %collective-permute-done.31 = bf16[1,1,1,2,2,192,384]{6,5,4,3,2,1,0:T(8,128)(2,1)S(1)} collective-permute-done((bf16[1,1,1,2,2,192,384]{6,5,4,3,2,1,0:T(8,128)(2,1)}, bf16[1,1,1,2,2,192,384]{6,5,4,3,2,1,0:T(8,128)(2,1)S(1)}, u32[]{:S(2)}, u32[]{:S(2)}) %collective-permute-start.31) | collective-permute-done | bytes 589856 | tf_op jit(solution)/shard_map/ppermute | solution.py:13
  339.7 4.4 add_bitcast_fusion.5
  355.0 2.3 copy.295
  357.3 2.3 copy.296
  372.3 2.4 copy.318
  374.6 2.3 collective-permute-done.25
  393.7 2.5 convolution_bitcast_fusion.7
  396.4 2.7 convolution_bitcast_fusion.6
  400.4 3.1 fusion.325
  434.8 2.5 convolution_bitcast_fusion.3
  439.4 2.5 convolution_bitcast_fusion.2
  477.9 56.5 %all_to_all.33 = bf16[2,1,1,4,2,384,384]{5,6,4,0,2,1,3:T(8,128)(2,1)S(1)} all-to-all(bf16[2,1,1,4,2,384,384]{5,6,4,0,2,1,3:T(8,128)(2,1)S(1)} %copy.339), channel_id=1, replica_groups=mesh['slab'=4,'kt'=8] {'slab'}, dimensions={3} | all-to-all | bytes 9437184 | tf_op jit(solution)/shard_map/all_to_all | solution.py:196
  536.3 4.3 copy.340
  540.6 2.6 copy.341
  (397 shorter events, 168.6 us)
Async XLA Ops:
  12.4 45.4 %all-to-all-start.1 = ((bf16[1,4,1,2,2,192,384]{6,5,4,3,2,0,1:T(8,128)(2,1)}), bf16[1,4,1,2,2,192,384]{6,5,4,3,2,0,1:T(8,128)(2,1)S(1)}, u32[]{:S(2)}, u32[]{:S(2)}) async-start(bf16[1,4,1,2,2,192,384]{6,5,4,3,2,0,1:T(8,128)(2,1)} %get-tuple-element.57), calls=%async_computation.1 | async-start | bytes 4718592 | tf_op jit(solution)/shard_map/all_to_all | solution.py:161
  16.6 376.3 %all-gather.5.cloned.1.call-start = ((), (), s32[]{:S(2)}) async-start(), calls=%async_computation.4 | async-start | bytes 2949120 | tf_op jit(solution)/shard_map/all_gather | solution.py:184
  59.2 32.1 %all-to-all-start = ((bf16[1,4,1,2,2,192,384]{6,5,4,3,2,0,1:T(8,128)(2,1)}), bf16[1,4,1,2,2,192,384]{6,5,4,3,2,0,1:T(8,128)(2,1)S(1)}, u32[]{:S(2)}, u32[]{:S(2)}) async-start(bf16[1,4,1,2,2,192,384]{6,5,4,3,2,0,1:T(8,128)(2,1)} %get-tuple-element.56), calls=%async_computation | async-start | bytes 4718592 | tf_op jit(solution)/shard_map/all_to_all | solution.py:161
  62.8 337.6 %all-gather.3.cloned.1.call-start = ((), (), s32[]{:S(2)}) async-start(), calls=%async_computation.3 | async-start | bytes 2949120 | tf_op jit(solution)/shard_map/all_gather | solution.py:183
  65.8 32.4 %collective-permute-start.6 = (bf16[1,1,1,2,2,192,384]{6,5,4,3,2,1,0:T(8,128)(2,1)}, bf16[1,1,1,2,2,192,384]{6,5,4,3,2,1,0:T(8,128)(2,1)}, u32[]{:S(2)}, u32[]{:S(2)}) collective-permute-start(bf16[1,1,1,2,2,192,384]{6,5,4,3,2,1,0:T(8,128)(2,1)} %get-tuple-element.77), channel_id=1, source_target_pairs={{0,7},{1,0},{2,1},{3,2},{4,3},{5,4},{6,5},{7,6},{8,15},{9,8},{10,9... | collective-permute-start | bytes 1769480 | tf_op jit(solution)/shard_map/ppermute | solution.py:13
  71.2 27.4 %collective-permute-start.7 = (bf16[1,1,1,2,2,192,384]{6,5,4,3,2,1,0:T(8,128)(2,1)}, bf16[1,1,1,2,2,192,384]{6,5,4,3,2,1,0:T(8,128)(2,1)}, u32[]{:S(2)}, u32[]{:S(2)}) collective-permute-start(bf16[1,1,1,2,2,192,384]{6,5,4,3,2,1,0:T(8,128)(2,1)} %get-tuple-element.77), channel_id=1, source_target_pairs={{0,6},{1,7},{2,0},{3,1},{4,2},{5,3},{6,4},{7,5},{8,14},{9,15},{10,... | collective-permute-start | bytes 1769480 | tf_op jit(solution)/shard_map/ppermute | solution.py:13
  71.6 27.7 %collective-permute-start.4 = (bf16[1,1,1,2,2,192,384]{6,5,4,3,2,1,0:T(8,128)(2,1)}, bf16[1,1,1,2,2,192,384]{6,5,4,3,2,1,0:T(8,128)(2,1)}, u32[]{:S(2)}, u32[]{:S(2)}) collective-permute-start(bf16[1,1,1,2,2,192,384]{6,5,4,3,2,1,0:T(8,128)(2,1)} %get-tuple-element.77), channel_id=1, source_target_pairs={{0,1},{1,2},{2,3},{3,4},{4,5},{5,6},{6,7},{7,0},{8,9},{9,10},{10,1... | collective-permute-start | bytes 1769480 | tf_op jit(solution)/shard_map/ppermute | solution.py:13
  72.2 39.2 %collective-permute-start.5 = (bf16[1,1,1,2,2,192,384]{6,5,4,3,2,1,0:T(8,128)(2,1)}, bf16[1,1,1,2,2,192,384]{6,5,4,3,2,1,0:T(8,128)(2,1)}, u32[]{:S(2)}, u32[]{:S(2)}) collective-permute-start(bf16[1,1,1,2,2,192,384]{6,5,4,3,2,1,0:T(8,128)(2,1)} %get-tuple-element.77), channel_id=1, source_target_pairs={{0,2},{1,3},{2,4},{3,5},{4,6},{5,7},{6,0},{7,1},{8,10},{9,11},{10,... | collective-permute-start | bytes 1769480 | tf_op jit(solution)/shard_map/ppermute | solution.py:13
  91.3 47.5 %copy-start.73 = (bf16[1,2,384,384]{3,2,1,0:T(8,128)(2,1)S(1)}, bf16[1,2,384,384]{3,2,1,0:T(8,128)(2,1)}, u32[]{:S(2)}) copy-start(bf16[1,2,384,384]{3,2,1,0:T(8,128)(2,1)} %param.13) | copy-start | bytes 1769476
  92.8 30.4 %collective-permute-start.2 = (bf16[1,1,1,2,2,192,384]{6,5,4,3,2,1,0:T(8,128)(2,1)}, bf16[1,1,1,2,2,192,384]{6,5,4,3,2,1,0:T(8,128)(2,1)S(1)}, u32[]{:S(2)}, u32[]{:S(2)}) collective-permute-start(bf16[1,1,1,2,2,192,384]{6,5,4,3,2,1,0:T(8,128)(2,1)} %get-tuple-element.73), channel_id=1, source_target_pairs={{0,7},{1,0},{2,1},{3,2},{4,3},{5,4},{6,5},{7,6},{8,15},{9,8},{10,9... | collective-permute-start | bytes 1769480 | tf_op jit(solution)/shard_map/ppermute | solution.py:13
  98.1 38.1 %collective-permute-start.3 = (bf16[1,1,1,2,2,192,384]{6,5,4,3,2,1,0:T(8,128)(2,1)}, bf16[1,1,1,2,2,192,384]{6,5,4,3,2,1,0:T(8,128)(2,1)S(1)}, u32[]{:S(2)}, u32[]{:S(2)}) collective-permute-start(bf16[1,1,1,2,2,192,384]{6,5,4,3,2,1,0:T(8,128)(2,1)} %get-tuple-element.73), channel_id=1, source_target_pairs={{0,6},{1,7},{2,0},{3,1},{4,2},{5,3},{6,4},{7,5},{8,14},{9,15},{10,... | collective-permute-start | bytes 1769480 | tf_op jit(solution)/shard_map/ppermute | solution.py:13
  98.6 38.6 %collective-permute-start = (bf16[1,1,1,2,2,192,384]{6,5,4,3,2,1,0:T(8,128)(2,1)}, bf16[1,1,1,2,2,192,384]{6,5,4,3,2,1,0:T(8,128)(2,1)S(1)}, u32[]{:S(2)}, u32[]{:S(2)}) collective-permute-start(bf16[1,1,1,2,2,192,384]{6,5,4,3,2,1,0:T(8,128)(2,1)} %get-tuple-element.73), channel_id=1, source_target_pairs={{0,1},{1,2},{2,3},{3,4},{4,5},{5,6},{6,7},{7,0},{8,9},{9,10},{10,1... | collective-permute-start | bytes 1769480 | tf_op jit(solution)/shard_map/ppermute | solution.py:13
  99.3 50.0 %collective-permute-start.1 = (bf16[1,1,1,2,2,192,384]{6,5,4,3,2,1,0:T(8,128)(2,1)}, bf16[1,1,1,2,2,192,384]{6,5,4,3,2,1,0:T(8,128)(2,1)S(1)}, u32[]{:S(2)}, u32[]{:S(2)}) collective-permute-start(bf16[1,1,1,2,2,192,384]{6,5,4,3,2,1,0:T(8,128)(2,1)} %get-tuple-element.73), channel_id=1, source_target_pairs={{0,2},{1,3},{2,4},{3,5},{4,6},{5,7},{6,0},{7,1},{8,10},{9,11},{10,... | collective-permute-start | bytes 1769480 | tf_op jit(solution)/shard_map/ppermute | solution.py:13
  111.5 49.6 %collective-permute-start.14 = (bf16[1,1,1,2,2,192,384]{6,5,4,3,2,1,0:T(8,128)(2,1)S(1)}, bf16[1,1,1,2,2,192,384]{6,5,4,3,2,1,0:T(8,128)(2,1)S(1)}, u32[]{:S(2)}, u32[]{:S(2)}) collective-permute-start(bf16[1,1,1,2,2,192,384]{6,5,4,3,2,1,0:T(8,128)(2,1)S(1)} %get-tuple-element.76), channel_id=1, source_target_pairs={{0,7},{1,0},{2,1},{3,2},{4,3},{5,4},{6,5},{7,6},{8,15},{9,8},{10,9... | collective-permute-start | bytes 1769480 | tf_op jit(solution)/shard_map/ppermute | solution.py:13
  123.2 15.6 %copy-start.74 = (bf16[1,1,1,2,2,192,384]{6,5,4,3,2,1,0:T(8,128)(2,1)}, bf16[1,1,1,2,2,192,384]{6,5,4,3,2,1,0:T(8,128)(2,1)S(1)}, u32[]{:S(2)}) copy-start(bf16[1,1,1,2,2,192,384]{6,5,4,3,2,1,0:T(8,128)(2,1)S(1)} %collective-permute-done.2) | copy-start | bytes 1769476
  123.2 51.1 %collective-permute-start.15 = (bf16[1,1,1,2,2,192,384]{6,5,4,3,2,1,0:T(8,128)(2,1)S(1)}, bf16[1,1,1,2,2,192,384]{6,5,4,3,2,1,0:T(8,128)(2,1)}, u32[]{:S(2)}, u32[]{:S(2)}) collective-permute-start(bf16[1,1,1,2,2,192,384]{6,5,4,3,2,1,0:T(8,128)(2,1)S(1)} %get-tuple-element.76), channel_id=1, source_target_pairs={{0,6},{1,7},{2,0},{3,1},{4,2},{5,3},{6,4},{7,5},{8,14},{9,15},{10,... | collective-permute-start | bytes 1769480 | tf_op jit(solution)/shard_map/ppermute | solution.py:13
  136.2 39.1 %collective-permute-start.12 = (bf16[1,1,1,2,2,192,384]{6,5,4,3,2,1,0:T(8,128)(2,1)S(1)}, bf16[1,1,1,2,2,192,384]{6,5,4,3,2,1,0:T(8,128)(2,1)}, u32[]{:S(2)}, u32[]{:S(2)}) collective-permute-start(bf16[1,1,1,2,2,192,384]{6,5,4,3,2,1,0:T(8,128)(2,1)S(1)} %get-tuple-element.76), channel_id=1, source_target_pairs={{0,1},{1,2},{2,3},{3,4},{4,5},{5,6},{6,7},{7,0},{8,9},{9,10},{10,1... | collective-permute-start | bytes 1769480 | tf_op jit(solution)/shard_map/ppermute | solution.py:13
  137.2 50.3 %collective-permute-start.13 = (bf16[1,1,1,2,2,192,384]{6,5,4,3,2,1,0:T(8,128)(2,1)S(1)}, bf16[1,1,1,2,2,192,384]{6,5,4,3,2,1,0:T(8,128)(2,1)}, u32[]{:S(2)}, u32[]{:S(2)}) collective-permute-start(bf16[1,1,1,2,2,192,384]{6,5,4,3,2,1,0:T(8,128)(2,1)S(1)} %get-tuple-element.76), channel_id=1, source_target_pairs={{0,2},{1,3},{2,4},{3,5},{4,6},{5,7},{6,0},{7,1},{8,10},{9,11},{10,... | collective-permute-start | bytes 1769480 | tf_op jit(solution)/shard_map/ppermute | solution.py:13
  149.4 42.0 %copy-start.80 = (bf16[1,1,1,2,2,192,384]{6,5,4,3,2,1,0:T(8,128)(2,1)}, bf16[1,1,1,2,2,192,384]{6,5,4,3,2,1,0:T(8,128)(2,1)S(1)}, u32[]{:S(2)}) copy-start(bf16[1,1,1,2,2,192,384]{6,5,4,3,2,1,0:T(8,128)(2,1)S(1)} %collective-permute-done.1) | copy-start | bytes 1769476
  149.4 52.7 %collective-permute-start.10 = (bf16[1,1,1,2,2,192,384]{6,5,4,3,2,1,0:T(8,128)(2,1)}, bf16[1,1,1,2,2,192,384]{6,5,4,3,2,1,0:T(8,128)(2,1)}, u32[]{:S(2)}, u32[]{:S(2)}) collective-permute-start(bf16[1,1,1,2,2,192,384]{6,5,4,3,2,1,0:T(8,128)(2,1)} %get-tuple-element.72), channel_id=1, source_target_pairs={{0,7},{1,0},{2,1},{3,2},{4,3},{5,4},{6,5},{7,6},{8,15},{9,8},{10,9... | collective-permute-start | bytes 1769480 | tf_op jit(solution)/shard_map/ppermute | solution.py:13
  161.0 26.4 %copy-start.82 = (bf16[1,1,1,2,2,192,384]{6,5,4,3,2,1,0:T(8,128)(2,1)}, bf16[1,1,1,2,2,192,384]{6,5,4,3,2,1,0:T(8,128)(2,1)S(1)}, u32[]{:S(2)}) copy-start(bf16[1,1,1,2,2,192,384]{6,5,4,3,2,1,0:T(8,128)(2,1)S(1)} %collective-permute-done.14) | copy-start | bytes 1769476
  161.1 51.1 %collective-permute-start.11 = (bf16[1,1,1,2,2,192,384]{6,5,4,3,2,1,0:T(8,128)(2,1)}, bf16[1,1,1,2,2,192,384]{6,5,4,3,2,1,0:T(8,128)(2,1)}, u32[]{:S(2)}, u32[]{:S(2)}) collective-permute-start(bf16[1,1,1,2,2,192,384]{6,5,4,3,2,1,0:T(8,128)(2,1)} %get-tuple-element.72), channel_id=1, source_target_pairs={{0,6},{1,7},{2,0},{3,1},{4,2},{5,3},{6,4},{7,5},{8,14},{9,15},{10,... | collective-permute-start | bytes 1769480 | tf_op jit(solution)/shard_map/ppermute | solution.py:13
  174.2 39.0 %collective-permute-start.8 = (bf16[1,1,1,2,2,192,384]{6,5,4,3,2,1,0:T(8,128)(2,1)}, bf16[1,1,1,2,2,192,384]{6,5,4,3,2,1,0:T(8,128)(2,1)}, u32[]{:S(2)}, u32[]{:S(2)}) collective-permute-start(bf16[1,1,1,2,2,192,384]{6,5,4,3,2,1,0:T(8,128)(2,1)} %get-tuple-element.72), channel_id=1, source_target_pairs={{0,1},{1,2},{2,3},{3,4},{4,5},{5,6},{6,7},{7,0},{8,9},{9,10},{10,1... | collective-permute-start | bytes 1769480 | tf_op jit(solution)/shard_map/ppermute | solution.py:13
  175.3 50.2 %collective-permute-start.9 = (bf16[1,1,1,2,2,192,384]{6,5,4,3,2,1,0:T(8,128)(2,1)}, bf16[1,1,1,2,2,192,384]{6,5,4,3,2,1,0:T(8,128)(2,1)}, u32[]{:S(2)}, u32[]{:S(2)}) collective-permute-start(bf16[1,1,1,2,2,192,384]{6,5,4,3,2,1,0:T(8,128)(2,1)} %get-tuple-element.72), channel_id=1, source_target_pairs={{0,2},{1,3},{2,4},{3,5},{4,6},{5,7},{6,0},{7,1},{8,10},{9,11},{10,... | collective-permute-start | bytes 1769480 | tf_op jit(solution)/shard_map/ppermute | solution.py:13
  187.5 49.6 %collective-permute-start.22 = (bf16[1,1,1,2,2,192,384]{6,5,4,3,2,1,0:T(8,128)(2,1)}, bf16[1,1,1,2,2,192,384]{6,5,4,3,2,1,0:T(8,128)(2,1)}, u32[]{:S(2)}, u32[]{:S(2)}) collective-permute-start(bf16[1,1,1,2,2,192,384]{6,5,4,3,2,1,0:T(8,128)(2,1)} %get-tuple-element.75), channel_id=1, source_target_pairs={{0,7},{1,0},{2,1},{3,2},{4,3},{5,4},{6,5},{7,6},{8,15},{9,8},{10,9... | collective-permute-start | bytes 1769480 | tf_op jit(solution)/shard_map/ppermute | solution.py:13
  192.9 9.0 %copy-start.97 = (f32[4]{0:T(128)S(1)}, f32[4]{0:T(128)}, u32[]{:S(2)}) copy-start(f32[4]{0:T(128)} %param.17) | copy-start | bytes 52
  202.0 57.9 %collective-permute-start.23 = (bf16[1,1,1,2,2,192,384]{6,5,4,3,2,1,0:T(8,128)(2,1)}, bf16[1,1,1,2,2,192,384]{6,5,4,3,2,1,0:T(8,128)(2,1)}, u32[]{:S(2)}, u32[]{:S(2)}) collective-permute-start(bf16[1,1,1,2,2,192,384]{6,5,4,3,2,1,0:T(8,128)(2,1)} %get-tuple-element.75), channel_id=1, source_target_pairs={{0,6},{1,7},{2,0},{3,1},{4,2},{5,3},{6,4},{7,5},{8,14},{9,15},{10,... | collective-permute-start | bytes 1769480 | tf_op jit(solution)/shard_map/ppermute | solution.py:13
  212.2 53.0 %collective-permute-start.20 = (bf16[1,1,1,2,2,192,384]{6,5,4,3,2,1,0:T(8,128)(2,1)}, bf16[1,1,1,2,2,192,384]{6,5,4,3,2,1,0:T(8,128)(2,1)}, u32[]{:S(2)}, u32[]{:S(2)}) collective-permute-start(bf16[1,1,1,2,2,192,384]{6,5,4,3,2,1,0:T(8,128)(2,1)} %get-tuple-element.75), channel_id=1, source_target_pairs={{0,1},{1,2},{2,3},{3,4},{4,5},{5,6},{6,7},{7,0},{8,9},{9,10},{10,1... | collective-permute-start | bytes 1769480 | tf_op jit(solution)/shard_map/ppermute | solution.py:13
  213.2 51.9 %collective-permute-start.21 = (bf16[1,1,1,2,2,192,384]{6,5,4,3,2,1,0:T(8,128)(2,1)}, bf16[1,1,1,2,2,192,384]{6,5,4,3,2,1,0:T(8,128)(2,1)}, u32[]{:S(2)}, u32[]{:S(2)}) collective-permute-start(bf16[1,1,1,2,2,192,384]{6,5,4,3,2,1,0:T(8,128)(2,1)} %get-tuple-element.75), channel_id=1, source_target_pairs={{0,2},{1,3},{2,4},{3,5},{4,6},{5,7},{6,0},{7,1},{8,10},{9,11},{10,... | collective-permute-start | bytes 1769480 | tf_op jit(solution)/shard_map/ppermute | solution.py:13
  225.5 49.6 %collective-permute-start.18 = (bf16[1,1,1,2,2,192,384]{6,5,4,3,2,1,0:T(8,128)(2,1)}, bf16[1,1,1,2,2,192,384]{6,5,4,3,2,1,0:T(8,128)(2,1)}, u32[]{:S(2)}, u32[]{:S(2)}) collective-permute-start(bf16[1,1,1,2,2,192,384]{6,5,4,3,2,1,0:T(8,128)(2,1)} %get-tuple-element.71), channel_id=1, source_target_pairs={{0,7},{1,0},{2,1},{3,2},{4,3},{5,4},{6,5},{7,6},{8,15},{9,8},{10,9... | collective-permute-start | bytes 1769480 | tf_op jit(solution)/shard_map/ppermute | solution.py:13
  237.1 50.9 %collective-permute-start.19 = (bf16[1,1,1,2,2,192,384]{6,5,4,3,2,1,0:T(8,128)(2,1)}, bf16[1,1,1,2,2,192,384]{6,5,4,3,2,1,0:T(8,128)(2,1)}, u32[]{:S(2)}, u32[]{:S(2)}) collective-permute-start(bf16[1,1,1,2,2,192,384]{6,5,4,3,2,1,0:T(8,128)(2,1)} %get-tuple-element.71), channel_id=1, source_target_pairs={{0,6},{1,7},{2,0},{3,1},{4,2},{5,3},{6,4},{7,5},{8,14},{9,15},{10,... | collective-permute-start | bytes 1769480 | tf_op jit(solution)/shard_map/ppermute | solution.py:13
  259.9 34.6 %collective-permute-start.16 = (bf16[1,1,1,2,2,192,384]{6,5,4,3,2,1,0:T(8,128)(2,1)}, bf16[1,1,1,2,2,192,384]{6,5,4,3,2,1,0:T(8,128)(2,1)S(1)}, u32[]{:S(2)}, u32[]{:S(2)}) collective-permute-start(bf16[1,1,1,2,2,192,384]{6,5,4,3,2,1,0:T(8,128)(2,1)} %get-tuple-element.71), channel_id=1, source_target_pairs={{0,1},{1,2},{2,3},{3,4},{4,5},{5,6},{6,7},{7,0},{8,9},{9,10},{10,1... | collective-permute-start | bytes 1769480 | tf_op jit(solution)/shard_map/ppermute | solution.py:13
  265.1 36.3 %collective-permute-start.17 = (bf16[1,1,1,2,2,192,384]{6,5,4,3,2,1,0:T(8,128)(2,1)}, bf16[1,1,1,2,2,192,384]{6,5,4,3,2,1,0:T(8,128)(2,1)S(1)}, u32[]{:S(2)}, u32[]{:S(2)}) collective-permute-start(bf16[1,1,1,2,2,192,384]{6,5,4,3,2,1,0:T(8,128)(2,1)} %get-tuple-element.71), channel_id=1, source_target_pairs={{0,2},{1,3},{2,4},{3,5},{4,6},{5,7},{6,0},{7,1},{8,10},{9,11},{10,... | collective-permute-start | bytes 1769480 | tf_op jit(solution)/shard_map/ppermute | solution.py:13
  265.1 47.9 %collective-permute-start.30 = (bf16[1,1,1,2,2,192,384]{6,5,4,3,2,1,0:T(8,128)(2,1)}, bf16[1,1,1,2,2,192,384]{6,5,4,3,2,1,0:T(8,128)(2,1)S(1)}, u32[]{:S(2)}, u32[]{:S(2)}) collective-permute-start(bf16[1,1,1,2,2,192,384]{6,5,4,3,2,1,0:T(8,128)(2,1)} %get-tuple-element.74), channel_id=1, source_target_pairs={{0,7},{1,0},{2,1},{3,2},{4,3},{5,4},{6,5},{7,6},{8,15},{9,8},{10,9... | collective-permute-start | bytes 1769480 | tf_op jit(solution)/shard_map/ppermute | solution.py:13
  275.1 50.7 %collective-permute-start.31 = (bf16[1,1,1,2,2,192,384]{6,5,4,3,2,1,0:T(8,128)(2,1)}, bf16[1,1,1,2,2,192,384]{6,5,4,3,2,1,0:T(8,128)(2,1)S(1)}, u32[]{:S(2)}, u32[]{:S(2)}) collective-permute-start(bf16[1,1,1,2,2,192,384]{6,5,4,3,2,1,0:T(8,128)(2,1)} %get-tuple-element.74), channel_id=1, source_target_pairs={{0,6},{1,7},{2,0},{3,1},{4,2},{5,3},{6,4},{7,5},{8,14},{9,15},{10,... | collective-permute-start | bytes 1769480 | tf_op jit(solution)/shard_map/ppermute | solution.py:13
  288.0 39.1 %collective-permute-start.28 = (bf16[1,1,1,2,2,192,384]{6,5,4,3,2,1,0:T(8,128)(2,1)}, bf16[1,1,1,2,2,192,384]{6,5,4,3,2,1,0:T(8,128)(2,1)S(1)}, u32[]{:S(2)}, u32[]{:S(2)}) collective-permute-start(bf16[1,1,1,2,2,192,384]{6,5,4,3,2,1,0:T(8,128)(2,1)} %get-tuple-element.74), channel_id=1, source_target_pairs={{0,1},{1,2},{2,3},{3,4},{4,5},{5,6},{6,7},{7,0},{8,9},{9,10},{10,1... | collective-permute-start | bytes 1769480 | tf_op jit(solution)/shard_map/ppermute | solution.py:13
  291.3 37.7 %copy-start.30 = (bf16[1,1,1,2,2,192,384]{5,6,4,3,2,1,0:T(8,128)(2,1)S(1)}, bf16[1,1,1,2,2,192,384]{5,6,4,3,2,1,0:T(8,128)(2,1)}, u32[]{:S(2)}) copy-start(bf16[1,1,1,2,2,192,384]{5,6,4,3,2,1,0:T(8,128)(2,1)} %copy.271) | copy-start | bytes 1769476
  291.3 37.7 %copy-start.31 = (bf16[1,1,1,2,2,192,384]{5,6,4,3,2,1,0:T(8,128)(2,1)S(1)}, bf16[1,1,1,2,2,192,384]{5,6,4,3,2,1,0:T(8,128)(2,1)}, u32[]{:S(2)}) copy-start(bf16[1,1,1,2,2,192,384]{5,6,4,3,2,1,0:T(8,128)(2,1)} %copy.272) | copy-start | bytes 1769476
  291.3 37.7 %copy-start.32 = (bf16[1,1,1,2,2,192,384]{5,6,4,3,2,1,0:T(8,128)(2,1)S(1)}, bf16[1,1,1,2,2,192,384]{5,6,4,3,2,1,0:T(8,128)(2,1)}, u32[]{:S(2)}) copy-start(bf16[1,1,1,2,2,192,384]{5,6,4,3,2,1,0:T(8,128)(2,1)} %copy.269) | copy-start | bytes 1769476
  291.3 37.7 %copy-start.33 = (bf16[1,1,1,2,2,192,384]{5,6,4,3,2,1,0:T(8,128)(2,1)S(1)}, bf16[1,1,1,2,2,192,384]{5,6,4,3,2,1,0:T(8,128)(2,1)}, u32[]{:S(2)}) copy-start(bf16[1,1,1,2,2,192,384]{5,6,4,3,2,1,0:T(8,128)(2,1)} %copy.270) | copy-start | bytes 1769476
  294.5 32.6 %copy-start.84 = (bf16[1,1,1,2,2,192,384]{6,5,4,3,2,1,0:T(8,128)(2,1)}, bf16[1,1,1,2,2,192,384]{6,5,4,3,2,1,0:T(8,128)(2,1)S(1)}, u32[]{:S(2)}) copy-start(bf16[1,1,1,2,2,192,384]{6,5,4,3,2,1,0:T(8,128)(2,1)S(1)} %collective-permute-done.16) | copy-start | bytes 1769476
  294.5 71.0 %collective-permute-start.29 = (bf16[1,1,1,2,2,192,384]{6,5,4,3,2,1,0:T(8,128)(2,1)}, bf16[1,1,1,2,2,192,384]{6,5,4,3,2,1,0:T(8,128)(2,1)}, u32[]{:S(2)}, u32[]{:S(2)}) collective-permute-start(bf16[1,1,1,2,2,192,384]{6,5,4,3,2,1,0:T(8,128)(2,1)} %get-tuple-element.74), channel_id=1, source_target_pairs={{0,2},{1,3},{2,4},{3,5},{4,6},{5,7},{6,0},{7,1},{8,10},{9,11},{10,... | collective-permute-start | bytes 1769480 | tf_op jit(solution)/shard_map/ppermute | solution.py:13
  301.4 27.6 %copy-start.86 = (bf16[1,1,1,2,2,192,384]{6,5,4,3,2,1,0:T(8,128)(2,1)}, bf16[1,1,1,2,2,192,384]{6,5,4,3,2,1,0:T(8,128)(2,1)S(1)}, u32[]{:S(2)}) copy-start(bf16[1,1,1,2,2,192,384]{6,5,4,3,2,1,0:T(8,128)(2,1)S(1)} %collective-permute-done.17) | copy-start | bytes 1769476
  301.4 66.4 %collective-permute-start.26 = (bf16[1,1,1,2,2,192,384]{6,5,4,3,2,1,0:T(8,128)(2,1)}, bf16[1,1,1,2,2,192,384]{6,5,4,3,2,1,0:T(8,128)(2,1)}, u32[]{:S(2)}, u32[]{:S(2)}) collective-permute-start(bf16[1,1,1,2,2,192,384]{6,5,4,3,2,1,0:T(8,128)(2,1)} %get-tuple-element.70), channel_id=1, source_target_pairs={{0,7},{1,0},{2,1},{3,2},{4,3},{5,4},{6,5},{7,6},{8,15},{9,8},{10,9... | collective-permute-start | bytes 1769480 | tf_op jit(solution)/shard_map/ppermute | solution.py:13
  313.1 15.9 %copy-start.88 = (bf16[1,1,1,2,2,192,384]{6,5,4,3,2,1,0:T(8,128)(2,1)}, bf16[1,1,1,2,2,192,384]{6,5,4,3,2,1,0:T(8,128)(2,1)S(1)}, u32[]{:S(2)}) copy-start(bf16[1,1,1,2,2,192,384]{6,5,4,3,2,1,0:T(8,128)(2,1)S(1)} %collective-permute-done.30) | copy-start | bytes 1769476
  313.1 57.0 %collective-permute-start.27 = (bf16[1,1,1,2,2,192,384]{6,5,4,3,2,1,0:T(8,128)(2,1)}, bf16[1,1,1,2,2,192,384]{6,5,4,3,2,1,0:T(8,128)(2,1)}, u32[]{:S(2)}, u32[]{:S(2)}) collective-permute-start(bf16[1,1,1,2,2,192,384]{6,5,4,3,2,1,0:T(8,128)(2,1)} %get-tuple-element.70), channel_id=1, source_target_pairs={{0,6},{1,7},{2,0},{3,1},{4,2},{5,3},{6,4},{7,5},{8,14},{9,15},{10,... | collective-permute-start | bytes 1769480 | tf_op jit(solution)/shard_map/ppermute | solution.py:13
  325.8 46.4 %collective-permute-start.24 = (bf16[1,1,1,2,2,192,384]{6,5,4,3,2,1,0:T(8,128)(2,1)}, bf16[1,1,1,2,2,192,384]{6,5,4,3,2,1,0:T(8,128)(2,1)}, u32[]{:S(2)}, u32[]{:S(2)}) collective-permute-start(bf16[1,1,1,2,2,192,384]{6,5,4,3,2,1,0:T(8,128)(2,1)} %get-tuple-element.70), channel_id=1, source_target_pairs={{0,1},{1,2},{2,3},{3,4},{4,5},{5,6},{6,7},{7,0},{8,9},{9,10},{10,1... | collective-permute-start | bytes 1769480 | tf_op jit(solution)/shard_map/ppermute | solution.py:13
  327.1 49.8 %collective-permute-start.25 = (bf16[1,1,1,2,2,192,384]{6,5,4,3,2,1,0:T(8,128)(2,1)}, bf16[1,1,1,2,2,192,384]{6,5,4,3,2,1,0:T(8,128)(2,1)}, u32[]{:S(2)}, u32[]{:S(2)}) collective-permute-start(bf16[1,1,1,2,2,192,384]{6,5,4,3,2,1,0:T(8,128)(2,1)} %get-tuple-element.70), channel_id=1, source_target_pairs={{0,2},{1,3},{2,4},{3,5},{4,6},{5,7},{6,0},{7,1},{8,10},{9,11},{10,... | collective-permute-start | bytes 1769480 | tf_op jit(solution)/shard_map/ppermute | solution.py:13
  (87 other events, 202.6 us)
Sparse Core Ops, SparseCore 0:
  19.0 39.4 all-gather.4
  138.9 24.6 all-gather.2
where the time goes:
time: 560 us; the launch traced here: 550 us
  waiting for transfers between devices  212 us (38%)
  local copies, waits for them, and re-layouts  120 us (21%)
  starting transfers between devices  61.8 us (11%)
  blocking collectives  61.7 us (11%)
  other arithmetic  49 us (9%)
  matrix products  28.9 us (5%)
  between operations  17.4 us (3%)
    ppermute x32, waiting for transfers between devices, from_behind(): lax.ppermute(value, axis, [(i, (i + by) % peers) for i in range(peers)])  152 us
    ppermute x32, local copies, waits for them, and re-layouts, from_behind(): lax.ppermute(value, axis, [(i, (i + by) % peers) for i in range(peers)])  59.5 us
    all_to_all x2, waiting for transfers between devices, body(): lax.all_to_all(previous[:, :, :, :, :, h * half:(h + 1) * half], 'slab',...  58.5 us
    all_to_all x1, blocking collectives, body(): lax.all_to_all(as_sent(jnp.stack([retarded_local, lesser_local])[:, None]...  56.5 us
    ppermute x32, starting transfers between devices, from_behind(): lax.ppermute(value, axis, [(i, (i + by) % peers) for i in range(peers)])  53.9 us
    unnamed x209, local copies, waits for them, and re-layouts  42.5 us
    add x8, other arithmetic, weigh(): strength[0] * behind.astype(jnp.float32)  20.3 us
    dot_general x8, matrix products, mul_adjoint(): jnp.einsum('...pij,qkj->...pqik', first_op, second_op, preferred_element_...  11.4 us
  transfers between devices with their start and end apart: 36, of which 23 were waited for; matrix products, arithmetic and copies ran while one was open for 19% of the time, Pallas kernels for 0%

commit v1 on v0

--- a/solution.py
+++ b/solution.py
@@ -6,6 +6,18 @@
 broaden = 0.05
 fermi_level = 0.0
 thermal = 0.1
+
+
+def cut_along(x, dim, size):
+    lengths = x.shape
+    pieces = x.reshape(*lengths[:dim], size, lengths[dim] // size, *lengths[dim + 1 :])
+    return jnp.moveaxis(pieces, dim, 0)
+
+
+def laid_out(pieces, dim):
+    pieces = jnp.moveaxis(pieces, 0, dim)
+    dims = pieces.shape
+    return pieces.reshape(*dims[:dim], dims[dim] * dims[dim + 1], *dims[dim + 2 :])
 
 
 def from_behind(value, axis, by):
@@ -193,13 +205,15 @@
         )
 
     retarded_local, lesser_local, unused = jax.vmap(run_whole)(initial, local_energies, phonon_all)
-    both_all = lax.all_to_all(
-        as_sent(jnp.stack([retarded_local, lesser_local])[:, None]),
-        "slab",
-        split_axis=3,
-        concat_axis=2,
-        tiled=True,
-    )
+    x = as_sent(jnp.stack([retarded_local, lesser_local])[:, None])
+    count, index = (lax.axis_size("slab"), lax.axis_index("slab"))
+    parts = cut_along(x, 3, count)
+    gathered = [parts[index]]
+    for step in range(1, count):
+        sent = parts[index ^ step]
+        gathered.append(lax.ppermute(sent, "slab", [(i_2, i_2 ^ step) for i_2 in range(count)]))
+    parts = jnp.stack(gathered)[index ^ jnp.arange(count)]
+    both_all = laid_out(parts, 2)
     return (both_all[0], both_all[1])
 
 

time: 560 us -> 575 us (1.027)
  starting transfers between devices: 61.8 us -> 164 us
  blocking collectives: 61.7 us -> 5.18 us
  waiting for transfers between devices: 212 us -> 171 us
  local copies, waits for them, and re-layouts: 120 us -> 129 us
    ppermute x32, waiting for transfers between devices: 152 us -> 61.9 us  [from_behind(): lax.ppermute(value, axis, [(i, (i + by) % peers) for i in range(peers)])]
    ppermute x32, starting transfers between devices: 53.9 us -> 144 us  [from_behind(): lax.ppermute(value, axis, [(i, (i + by) % peers) for i in range(peers)])]
    all_to_all x1 -> x0, blocking collectives: 56.5 us -> none  [body(): lax.all_to_all(as_sent(jnp.stack([retarded_local, lesser_local])[:, None]...]
    ppermute x0 -> x3, waiting for transfers between devices: none -> 49.7 us  [body(): lax.ppermute(sent, 'slab', [(i_2, i_2 ^ step) for i_2 in range(count)])]
    ppermute x0 -> x3, starting transfers between devices: none -> 11.8 us  [body(): lax.ppermute(sent, 'slab', [(i_2, i_2 ^ step) for i_2 in range(count)])]
    gather x0 -> x1, local copies, waits for them, and re-layouts: none -> 5.78 us  [body(): parts = jnp.stack(gathered)[index ^ jnp.arange(count)]]
    unnamed x209 -> x216, local copies, waits for them, and re-layouts: 42.5 us -> 42.5 us
  transfers between devices with their start and end apart: 36 -> 39, of which waited for: 23 -> 15; matrix products, arithmetic and copies ran while one was open for 19% -> 19% of each run, Pallas kernels for 0% -> 0%
where the time goes in v1:
time: 575 us; the launch traced here: 565 us
  waiting for transfers between devices  171 us (30%)
  starting transfers between devices  164 us (29%)
  local copies, waits for them, and re-layouts  129 us (22%)
  other arithmetic  52.3 us (9%)
  matrix products  26.4 us (5%)
  between operations  17.5 us (3%)
    ppermute x32, starting transfers between devices, from_behind(): lax.ppermute(value, axis, [(i, (i + by) % peers) for i in range(peers)])  144 us
    ppermute x32, waiting for transfers between devices, from_behind(): lax.ppermute(value, axis, [(i, (i + by) % peers) for i in range(peers)])  61.9 us
    ppermute x32, local copies, waits for them, and re-layouts, from_behind(): lax.ppermute(value, axis, [(i, (i + by) % peers) for i in range(peers)])  59.5 us
    all_to_all x2, waiting for transfers between devices, body(): lax.all_to_all(previous[:, :, :, :, :, h * half:(h + 1) * half], 'slab',...  58.3 us
    ppermute x3, waiting for transfers between devices, body(): lax.ppermute(sent, 'slab', [(i_2, i_2 ^ step) for i_2 in range(count)])  49.7 us
    unnamed x216, local copies, waits for them, and re-layouts  42.5 us
    add x8, other arithmetic, weigh(): strength[0] * behind.astype(jnp.float32)  19.2 us
    ppermute x3, starting transfers between devices, body(): lax.ppermute(sent, 'slab', [(i_2, i_2 ^ step) for i_2 in range(count)])  11.8 us
  transfers between devices with their start and end apart: 39, of which 15 were waited for; matrix products, arithmetic and copies ran while one was open for 19% of the time, Pallas kernels for 0%

profile of v1, /device:TPU:0, one launch (start us, length us, event | category | flops | bytes accessed | tf_op | source)
XLA Modules:
  0.0 565.0 jit_solution(1886322497805391101)
XLA Ops:
  7.2 5.2 fusion.330
  12.4 4.2 all-to-all-start
  17.4 40.4 %all-to-all-done = bf16[1,4,1,2,2,192,384]{6,5,4,3,2,0,1:T(8,128)(2,1)S(1)} async-done(((bf16[1,4,1,2,2,192,384]{6,5,4,3,2,0,1:T(8,128)(2,1)}), bf16[1,4,1,2,2,192,384]{6,5,4,3,2,0,1:T(8,128)(2,1)S(1)}, u32[]{:S(2)}, u32[]{:S(2)}) %all-to-all-start) | async-done | bytes 2359328 | tf_op jit(solution)/shard_map/all_to_all | solution.py:173
  59.2 3.6 all-to-all-start.1
  62.9 3.1 fusion.332
  66.0 2.3 collective-permute-start
  69.9 3.2 collective-permute-start.2
  73.4 17.9 %all-to-all-done.1 = bf16[1,4,1,2,2,192,384]{6,5,4,3,2,0,1:T(8,128)(2,1)S(1)} async-done(((bf16[1,4,1,2,2,192,384]{6,5,4,3,2,0,1:T(8,128)(2,1)}), bf16[1,4,1,2,2,192,384]{6,5,4,3,2,0,1:T(8,128)(2,1)S(1)}, u32[]{:S(2)}, u32[]{:S(2)}) %all-to-all-start.1) | async-done | bytes 2359328 | tf_op jit(solution)/shard_map/all_to_all | solution.py:173
  92.6 2.3 collective-permute-start.4
  96.5 16.0 %collective-permute-start.6 = (bf16[1,1,1,2,2,192,384]{6,5,4,3,2,1,0:T(8,128)(2,1)}, bf16[1,1,1,2,2,192,384]{6,5,4,3,2,1,0:T(8,128)(2,1)S(1)}, u32[]{:S(2)}, u32[]{:S(2)}) collective-permute-start(bf16[1,1,1,2,2,192,384]{6,5,4,3,2,1,0:T(8,128)(2,1)} %get-tuple-element.85), channel_id=1, source_target_pairs={{0,7},{1,0},{2,1},{3,2},{4,3},{5,4},{6,5},{7,6},{8,15},{9,8},{10,9... | collective-permute-start | bytes 1769480 | tf_op jit(solution)/shard_map/ppermute | solution.py:25
  114.5 9.3 %collective-permute-done.4 = bf16[1,1,1,2,2,192,384]{6,5,4,3,2,1,0:T(8,128)(2,1)S(1)} collective-permute-done((bf16[1,1,1,2,2,192,384]{6,5,4,3,2,1,0:T(8,128)(2,1)}, bf16[1,1,1,2,2,192,384]{6,5,4,3,2,1,0:T(8,128)(2,1)S(1)}, u32[]{:S(2)}, u32[]{:S(2)}) %collective-permute-start.4) | collective-permute-done | bytes 589856 | tf_op jit(solution)/shard_map/ppermute | solution.py:25
  124.5 25.7 %collective-permute-start.14 = (bf16[1,1,1,2,2,192,384]{6,5,4,3,2,1,0:T(8,128)(2,1)S(1)}, bf16[1,1,1,2,2,192,384]{6,5,4,3,2,1,0:T(8,128)(2,1)}, u32[]{:S(2)}, u32[]{:S(2)}) collective-permute-start(bf16[1,1,1,2,2,192,384]{6,5,4,3,2,1,0:T(8,128)(2,1)S(1)} %get-tuple-element.84), channel_id=1, source_target_pairs={{0,7},{1,0},{2,1},{3,2},{4,3},{5,4},{6,5},{7,6},{8,15},{9,8},{10,9... | collective-permute-start | bytes 1769480 | tf_op jit(solution)/shard_map/ppermute | solution.py:25
  152.4 9.4 %collective-permute-done.12 = bf16[1,1,1,2,2,192,384]{6,5,4,3,2,1,0:T(8,128)(2,1)S(1)} collective-permute-done((bf16[1,1,1,2,2,192,384]{6,5,4,3,2,1,0:T(8,128)(2,1)S(1)}, bf16[1,1,1,2,2,192,384]{6,5,4,3,2,1,0:T(8,128)(2,1)S(1)}, u32[]{:S(2)}, u32[]{:S(2)}) %collective-permute-start.12) | collective-permute-done | bytes 589856 | tf_op jit(solution)/shard_map/ppermute | solution.py:25
  162.6 25.6 %collective-permute-start.10 = (bf16[1,1,1,2,2,192,384]{6,5,4,3,2,1,0:T(8,128)(2,1)}, bf16[1,1,1,2,2,192,384]{6,5,4,3,2,1,0:T(8,128)(2,1)}, u32[]{:S(2)}, u32[]{:S(2)}) collective-permute-start(bf16[1,1,1,2,2,192,384]{6,5,4,3,2,1,0:T(8,128)(2,1)} %get-tuple-element.80), channel_id=1, source_target_pairs={{0,7},{1,0},{2,1},{3,2},{4,3},{5,4},{6,5},{7,6},{8,15},{9,8},{10,9... | collective-permute-start | bytes 1769480 | tf_op jit(solution)/shard_map/ppermute | solution.py:25
  195.4 5.2 all_gather.9
  201.6 24.5 %collective-permute-start.22 = (bf16[1,1,1,2,2,192,384]{6,5,4,3,2,1,0:T(8,128)(2,1)}, bf16[1,1,1,2,2,192,384]{6,5,4,3,2,1,0:T(8,128)(2,1)}, u32[]{:S(2)}, u32[]{:S(2)}) collective-permute-start(bf16[1,1,1,2,2,192,384]{6,5,4,3,2,1,0:T(8,128)(2,1)} %get-tuple-element.83), channel_id=1, source_target_pairs={{0,7},{1,0},{2,1},{3,2},{4,3},{5,4},{6,5},{7,6},{8,15},{9,8},{10,9... | collective-permute-start | bytes 1769480 | tf_op jit(solution)/shard_map/ppermute | solution.py:25
  226.7 11.0 %collective-permute-done.20 = bf16[1,1,1,2,2,192,384]{6,5,4,3,2,1,0:T(8,128)(2,1)} collective-permute-done((bf16[1,1,1,2,2,192,384]{6,5,4,3,2,1,0:T(8,128)(2,1)}, bf16[1,1,1,2,2,192,384]{6,5,4,3,2,1,0:T(8,128)(2,1)}, u32[]{:S(2)}, u32[]{:S(2)}) %collective-permute-start.20) | collective-permute-done | bytes 589856 | tf_op jit(solution)/shard_map/ppermute | solution.py:25
  242.9 2.3 copy.400
  245.2 2.3 copy.401
  253.3 2.3 copy.431
  255.6 2.3 copy.432
  260.1 4.0 collective-permute-start.18
  265.9 9.9 %collective-permute-done.16 = bf16[1,1,1,2,2,192,384]{6,5,4,3,2,1,0:T(8,128)(2,1)} collective-permute-done((bf16[1,1,1,2,2,192,384]{6,5,4,3,2,1,0:T(8,128)(2,1)}, bf16[1,1,1,2,2,192,384]{6,5,4,3,2,1,0:T(8,128)(2,1)}, u32[]{:S(2)}, u32[]{:S(2)}) %collective-permute-start.16) | collective-permute-done | bytes 589856 | tf_op jit(solution)/shard_map/ppermute | solution.py:25
  276.7 13.8 %collective-permute-start.30 = (bf16[1,1,1,2,2,192,384]{6,5,4,3,2,1,0:T(8,128)(2,1)}, bf16[1,1,1,2,2,192,384]{6,5,4,3,2,1,0:T(8,128)(2,1)S(1)}, u32[]{:S(2)}, u32[]{:S(2)}) collective-permute-start(bf16[1,1,1,2,2,192,384]{6,5,4,3,2,1,0:T(8,128)(2,1)} %get-tuple-element.82), channel_id=1, source_target_pairs={{0,7},{1,0},{2,1},{3,2},{4,3},{5,4},{6,5},{7,6},{8,15},{9,8},{10,9... | collective-permute-start | bytes 1769480 | tf_op jit(solution)/shard_map/ppermute | solution.py:25
  290.4 3.1 add_bitcast_fusion.7
  293.6 3.1 add_bitcast_fusion.6
  297.0 4.6 collective-permute-done.19
  301.6 12.0 %collective-permute-done.28 = bf16[1,1,1,2,2,192,384]{6,5,4,3,2,1,0:T(8,128)(2,1)S(1)} collective-permute-done((bf16[1,1,1,2,2,192,384]{6,5,4,3,2,1,0:T(8,128)(2,1)}, bf16[1,1,1,2,2,192,384]{6,5,4,3,2,1,0:T(8,128)(2,1)S(1)}, u32[]{:S(2)}, u32[]{:S(2)}) %collective-permute-start.28) | collective-permute-done | bytes 589856 | tf_op jit(solution)/shard_map/ppermute | solution.py:25
  314.6 13.7 %collective-permute-start.26 = (bf16[1,1,1,2,2,192,384]{6,5,4,3,2,1,0:T(8,128)(2,1)}, bf16[1,1,1,2,2,192,384]{6,5,4,3,2,1,0:T(8,128)(2,1)}, u32[]{:S(2)}, u32[]{:S(2)}) collective-permute-start(bf16[1,1,1,2,2,192,384]{6,5,4,3,2,1,0:T(8,128)(2,1)} %get-tuple-element.78), channel_id=1, source_target_pairs={{0,7},{1,0},{2,1},{3,2},{4,3},{5,4},{6,5},{7,6},{8,15},{9,8},{10,9... | collective-permute-start | bytes 1769480 | tf_op jit(solution)/shard_map/ppermute | solution.py:25
  333.0 2.3 copy.427
  337.5 2.3 copy.429
  339.7 4.3 add_bitcast_fusion.5
  354.9 2.3 copy.454
  357.2 2.3 copy.455
  365.4 2.3 copy.486
  369.8 2.3 copy.480
  372.1 2.3 copy.481
  374.4 2.5 collective-permute-done.27
  393.1 2.5 convolution_bitcast_fusion.7
  395.8 2.7 convolution_bitcast_fusion.6
  399.9 3.0 fusion.331
  475.7 2.4 copy.501
  479.6 11.6 %collective-permute-start.33 = (bf16[2,1,1,1,2,384,384]{6,5,4,0,3,2,1:T(8,128)(2,1)}, bf16[2,1,1,1,2,384,384]{6,5,4,0,3,2,1:T(8,128)(2,1)S(1)}, u32[]{:S(2)}, u32[]{:S(2)}) collective-permute-start(bf16[2,1,1,1,2,384,384]{6,5,4,0,3,2,1:T(8,128)(2,1)} %bitcast.1000), channel_id=1, source_target_pairs={{0,16},{8,24},{16,0},{24,8},{1,17},{9,25},{17,1},{25,9},{2,18},{10... | collective-permute-start | bytes 3538952 | tf_op jit(solution)/shard_map/ppermute | solution.py:214
  493.6 24.7 %collective-permute-done.33 = bf16[2,1,1,1,2,384,384]{6,5,4,0,3,2,1:T(8,128)(2,1)S(1)} collective-permute-done((bf16[2,1,1,1,2,384,384]{6,5,4,0,3,2,1:T(8,128)(2,1)}, bf16[2,1,1,1,2,384,384]{6,5,4,0,3,2,1:T(8,128)(2,1)S(1)}, u32[]{:S(2)}, u32[]{:S(2)}) %collective-permute-start.33) | collective-permute-done | bytes 1179680 | tf_op jit(solution)/shard_map/ppermute | solution.py:214
  518.2 25.0 %collective-permute-done.34 = bf16[2,1,1,1,2,384,384]{6,5,4,0,3,2,1:T(8,128)(2,1)} collective-permute-done((bf16[2,1,1,1,2,384,384]{6,5,4,0,3,2,1:T(8,128)(2,1)}, bf16[2,1,1,1,2,384,384]{6,5,4,0,3,2,1:T(8,128)(2,1)}, u32[]{:S(2)}, u32[]{:S(2)}) %collective-permute-start.34) | collective-permute-done | bytes 1179680 | tf_op jit(solution)/shard_map/ppermute | solution.py:214
  543.2 3.8 maximum_bitcast_fusion
  547.0 5.8 %gather_fusion = bf16[4,2,2,384,384]{4,3,2,1,0:T(8,128)(2,1)} fusion(bf16[4,2,2,384,384]{4,3,2,1,0:T(8,128)(2,1)} %maximum_bitcast_fusion, s32[1024]{0:T(1024)S(1)} %pad_clamp_fusion), kind=kCustom, calls=%fused_computation | custom fusion | bytes 9437200 | tf_op jit(solution)/shard_map/gather | solution.py:215
  552.8 5.2 slice_bitcast_fusion
  (415 shorter events, 155.8 us)
Async XLA Ops:
  12.4 45.4 %all-to-all-start = ((bf16[1,4,1,2,2,192,384]{6,5,4,3,2,0,1:T(8,128)(2,1)}), bf16[1,4,1,2,2,192,384]{6,5,4,3,2,0,1:T(8,128)(2,1)S(1)}, u32[]{:S(2)}, u32[]{:S(2)}) async-start(bf16[1,4,1,2,2,192,384]{6,5,4,3,2,0,1:T(8,128)(2,1)} %get-tuple-element.62), calls=%async_computation | async-start | bytes 4718592 | tf_op jit(solution)/shard_map/all_to_all | solution.py:173
  16.6 375.7 %all-gather.5.cloned.1.call-start = ((), (), s32[]{:S(2)}) async-start(), calls=%async_computation.3 | async-start | bytes 2949120 | tf_op jit(solution)/shard_map/all_gather | solution.py:196
  59.2 32.1 %all-to-all-start.1 = ((bf16[1,4,1,2,2,192,384]{6,5,4,3,2,0,1:T(8,128)(2,1)}), bf16[1,4,1,2,2,192,384]{6,5,4,3,2,0,1:T(8,128)(2,1)S(1)}, u32[]{:S(2)}, u32[]{:S(2)}) async-start(bf16[1,4,1,2,2,192,384]{6,5,4,3,2,0,1:T(8,128)(2,1)} %get-tuple-element.63), calls=%async_computation.1 | async-start | bytes 4718592 | tf_op jit(solution)/shard_map/all_to_all | solution.py:173
  62.8 337.0 %all-gather.3.cloned.1.call-start = ((), (), s32[]{:S(2)}) async-start(), calls=%async_computation.2 | async-start | bytes 2949120 | tf_op jit(solution)/shard_map/all_gather | solution.py:195
  66.0 28.9 %collective-permute-start = (bf16[1,1,1,2,2,192,384]{6,5,4,3,2,1,0:T(8,128)(2,1)}, bf16[1,1,1,2,2,192,384]{6,5,4,3,2,1,0:T(8,128)(2,1)}, u32[]{:S(2)}, u32[]{:S(2)}) collective-permute-start(bf16[1,1,1,2,2,192,384]{6,5,4,3,2,1,0:T(8,128)(2,1)} %get-tuple-element.81), channel_id=1, source_target_pairs={{0,1},{1,2},{2,3},{3,4},{4,5},{5,6},{6,7},{7,0},{8,9},{9,10},{10,1... | collective-permute-start | bytes 1769480 | tf_op jit(solution)/shard_map/ppermute | solution.py:25
  68.3 28.2 %collective-permute-start.1 = (bf16[1,1,1,2,2,192,384]{6,5,4,3,2,1,0:T(8,128)(2,1)}, bf16[1,1,1,2,2,192,384]{6,5,4,3,2,1,0:T(8,128)(2,1)}, u32[]{:S(2)}, u32[]{:S(2)}) collective-permute-start(bf16[1,1,1,2,2,192,384]{6,5,4,3,2,1,0:T(8,128)(2,1)} %get-tuple-element.81), channel_id=1, source_target_pairs={{0,2},{1,3},{2,4},{3,5},{4,6},{5,7},{6,0},{7,1},{8,10},{9,11},{10,... | collective-permute-start | bytes 1769480 | tf_op jit(solution)/shard_map/ppermute | solution.py:25
  69.9 42.6 %collective-permute-start.2 = (bf16[1,1,1,2,2,192,384]{6,5,4,3,2,1,0:T(8,128)(2,1)}, bf16[1,1,1,2,2,192,384]{6,5,4,3,2,1,0:T(8,128)(2,1)}, u32[]{:S(2)}, u32[]{:S(2)}) collective-permute-start(bf16[1,1,1,2,2,192,384]{6,5,4,3,2,1,0:T(8,128)(2,1)} %get-tuple-element.81), channel_id=1, source_target_pairs={{0,7},{1,0},{2,1},{3,2},{4,3},{5,4},{6,5},{7,6},{8,15},{9,8},{10,9... | collective-permute-start | bytes 1769480 | tf_op jit(solution)/shard_map/ppermute | solution.py:25
  73.1 39.6 %collective-permute-start.3 = (bf16[1,1,1,2,2,192,384]{6,5,4,3,2,1,0:T(8,128)(2,1)}, bf16[1,1,1,2,2,192,384]{6,5,4,3,2,1,0:T(8,128)(2,1)}, u32[]{:S(2)}, u32[]{:S(2)}) collective-permute-start(bf16[1,1,1,2,2,192,384]{6,5,4,3,2,1,0:T(8,128)(2,1)} %get-tuple-element.81), channel_id=1, source_target_pairs={{0,6},{1,7},{2,0},{3,1},{4,2},{5,3},{6,4},{7,5},{8,14},{9,15},{10,... | collective-permute-start | bytes 1769480 | tf_op jit(solution)/shard_map/ppermute | solution.py:25
  91.3 59.8 %copy-start.77 = (bf16[1,2,384,384]{3,2,1,0:T(8,128)(2,1)S(1)}, bf16[1,2,384,384]{3,2,1,0:T(8,128)(2,1)}, u32[]{:S(2)}) copy-start(bf16[1,2,384,384]{3,2,1,0:T(8,128)(2,1)} %param.13) | copy-start | bytes 1769476
  92.6 31.2 %collective-permute-start.4 = (bf16[1,1,1,2,2,192,384]{6,5,4,3,2,1,0:T(8,128)(2,1)}, bf16[1,1,1,2,2,192,384]{6,5,4,3,2,1,0:T(8,128)(2,1)S(1)}, u32[]{:S(2)}, u32[]{:S(2)}) collective-permute-start(bf16[1,1,1,2,2,192,384]{6,5,4,3,2,1,0:T(8,128)(2,1)} %get-tuple-element.85), channel_id=1, source_target_pairs={{0,1},{1,2},{2,3},{3,4},{4,5},{5,6},{6,7},{7,0},{8,9},{9,10},{10,1... | collective-permute-start | bytes 1769480 | tf_op jit(solution)/shard_map/ppermute | solution.py:25
  94.9 29.6 %collective-permute-start.5 = (bf16[1,1,1,2,2,192,384]{6,5,4,3,2,1,0:T(8,128)(2,1)}, bf16[1,1,1,2,2,192,384]{6,5,4,3,2,1,0:T(8,128)(2,1)S(1)}, u32[]{:S(2)}, u32[]{:S(2)}) collective-permute-start(bf16[1,1,1,2,2,192,384]{6,5,4,3,2,1,0:T(8,128)(2,1)} %get-tuple-element.85), channel_id=1, source_target_pairs={{0,2},{1,3},{2,4},{3,5},{4,6},{5,7},{6,0},{7,1},{8,10},{9,11},{10,... | collective-permute-start | bytes 1769480 | tf_op jit(solution)/shard_map/ppermute | solution.py:25
  96.5 53.8 %collective-permute-start.6 = (bf16[1,1,1,2,2,192,384]{6,5,4,3,2,1,0:T(8,128)(2,1)}, bf16[1,1,1,2,2,192,384]{6,5,4,3,2,1,0:T(8,128)(2,1)S(1)}, u32[]{:S(2)}, u32[]{:S(2)}) collective-permute-start(bf16[1,1,1,2,2,192,384]{6,5,4,3,2,1,0:T(8,128)(2,1)} %get-tuple-element.85), channel_id=1, source_target_pairs={{0,7},{1,0},{2,1},{3,2},{4,3},{5,4},{6,5},{7,6},{8,15},{9,8},{10,9... | collective-permute-start | bytes 1769480 | tf_op jit(solution)/shard_map/ppermute | solution.py:25
  112.4 38.7 %collective-permute-start.7 = (bf16[1,1,1,2,2,192,384]{6,5,4,3,2,1,0:T(8,128)(2,1)}, bf16[1,1,1,2,2,192,384]{6,5,4,3,2,1,0:T(8,128)(2,1)S(1)}, u32[]{:S(2)}, u32[]{:S(2)}) collective-permute-start(bf16[1,1,1,2,2,192,384]{6,5,4,3,2,1,0:T(8,128)(2,1)} %get-tuple-element.85), channel_id=1, source_target_pairs={{0,6},{1,7},{2,0},{3,1},{4,2},{5,3},{6,4},{7,5},{8,14},{9,15},{10,... | collective-permute-start | bytes 1769480 | tf_op jit(solution)/shard_map/ppermute | solution.py:25
  112.7 49.1 %collective-permute-start.12 = (bf16[1,1,1,2,2,192,384]{6,5,4,3,2,1,0:T(8,128)(2,1)S(1)}, bf16[1,1,1,2,2,192,384]{6,5,4,3,2,1,0:T(8,128)(2,1)S(1)}, u32[]{:S(2)}, u32[]{:S(2)}) collective-permute-start(bf16[1,1,1,2,2,192,384]{6,5,4,3,2,1,0:T(8,128)(2,1)S(1)} %get-tuple-element.84), channel_id=1, source_target_pairs={{0,1},{1,2},{2,3},{3,4},{4,5},{5,6},{6,7},{7,0},{8,9},{9,10},{10,1... | collective-permute-start | bytes 1769480 | tf_op jit(solution)/shard_map/ppermute | solution.py:25
  123.8 26.7 %copy-start.78 = (bf16[1,1,1,2,2,192,384]{6,5,4,3,2,1,0:T(8,128)(2,1)}, bf16[1,1,1,2,2,192,384]{6,5,4,3,2,1,0:T(8,128)(2,1)S(1)}, u32[]{:S(2)}) copy-start(bf16[1,1,1,2,2,192,384]{6,5,4,3,2,1,0:T(8,128)(2,1)S(1)} %collective-permute-done.4) | copy-start | bytes 1769476
  123.8 38.8 %collective-permute-start.13 = (bf16[1,1,1,2,2,192,384]{6,5,4,3,2,1,0:T(8,128)(2,1)S(1)}, bf16[1,1,1,2,2,192,384]{6,5,4,3,2,1,0:T(8,128)(2,1)}, u32[]{:S(2)}, u32[]{:S(2)}) collective-permute-start(bf16[1,1,1,2,2,192,384]{6,5,4,3,2,1,0:T(8,128)(2,1)S(1)} %get-tuple-element.84), channel_id=1, source_target_pairs={{0,2},{1,3},{2,4},{3,5},{4,6},{5,7},{6,0},{7,1},{8,10},{9,11},{10,... | collective-permute-start | bytes 1769480 | tf_op jit(solution)/shard_map/ppermute | solution.py:25
  124.5 63.7 %collective-permute-start.14 = (bf16[1,1,1,2,2,192,384]{6,5,4,3,2,1,0:T(8,128)(2,1)S(1)}, bf16[1,1,1,2,2,192,384]{6,5,4,3,2,1,0:T(8,128)(2,1)}, u32[]{:S(2)}, u32[]{:S(2)}) collective-permute-start(bf16[1,1,1,2,2,192,384]{6,5,4,3,2,1,0:T(8,128)(2,1)S(1)} %get-tuple-element.84), channel_id=1, source_target_pairs={{0,7},{1,0},{2,1},{3,2},{4,3},{5,4},{6,5},{7,6},{8,15},{9,8},{10,9... | collective-permute-start | bytes 1769480 | tf_op jit(solution)/shard_map/ppermute | solution.py:25
  150.2 38.0 %collective-permute-start.15 = (bf16[1,1,1,2,2,192,384]{6,5,4,3,2,1,0:T(8,128)(2,1)S(1)}, bf16[1,1,1,2,2,192,384]{6,5,4,3,2,1,0:T(8,128)(2,1)}, u32[]{:S(2)}, u32[]{:S(2)}) collective-permute-start(bf16[1,1,1,2,2,192,384]{6,5,4,3,2,1,0:T(8,128)(2,1)S(1)} %get-tuple-element.84), channel_id=1, source_target_pairs={{0,6},{1,7},{2,0},{3,1},{4,2},{5,3},{6,4},{7,5},{8,14},{9,15},{10,... | collective-permute-start | bytes 1769480 | tf_op jit(solution)/shard_map/ppermute | solution.py:25
  151.2 38.9 %copy-start.84 = (bf16[1,1,1,2,2,192,384]{6,5,4,3,2,1,0:T(8,128)(2,1)}, bf16[1,1,1,2,2,192,384]{6,5,4,3,2,1,0:T(8,128)(2,1)S(1)}, u32[]{:S(2)}) copy-start(bf16[1,1,1,2,2,192,384]{6,5,4,3,2,1,0:T(8,128)(2,1)S(1)} %collective-permute-done.7) | copy-start | bytes 1769476
  151.2 49.5 %collective-permute-start.8 = (bf16[1,1,1,2,2,192,384]{6,5,4,3,2,1,0:T(8,128)(2,1)}, bf16[1,1,1,2,2,192,384]{6,5,4,3,2,1,0:T(8,128)(2,1)}, u32[]{:S(2)}, u32[]{:S(2)}) collective-permute-start(bf16[1,1,1,2,2,192,384]{6,5,4,3,2,1,0:T(8,128)(2,1)} %get-tuple-element.80), channel_id=1, source_target_pairs={{0,1},{1,2},{2,3},{3,4},{4,5},{5,6},{6,7},{7,0},{8,9},{9,10},{10,1... | collective-permute-start | bytes 1769480 | tf_op jit(solution)/shard_map/ppermute | solution.py:25
  161.8 39.9 %collective-permute-start.9 = (bf16[1,1,1,2,2,192,384]{6,5,4,3,2,1,0:T(8,128)(2,1)}, bf16[1,1,1,2,2,192,384]{6,5,4,3,2,1,0:T(8,128)(2,1)}, u32[]{:S(2)}, u32[]{:S(2)}) collective-permute-start(bf16[1,1,1,2,2,192,384]{6,5,4,3,2,1,0:T(8,128)(2,1)} %get-tuple-element.80), channel_id=1, source_target_pairs={{0,2},{1,3},{2,4},{3,5},{4,6},{5,7},{6,0},{7,1},{8,10},{9,11},{10,... | collective-permute-start | bytes 1769480 | tf_op jit(solution)/shard_map/ppermute | solution.py:25
  162.6 63.5 %collective-permute-start.10 = (bf16[1,1,1,2,2,192,384]{6,5,4,3,2,1,0:T(8,128)(2,1)}, bf16[1,1,1,2,2,192,384]{6,5,4,3,2,1,0:T(8,128)(2,1)}, u32[]{:S(2)}, u32[]{:S(2)}) collective-permute-start(bf16[1,1,1,2,2,192,384]{6,5,4,3,2,1,0:T(8,128)(2,1)} %get-tuple-element.80), channel_id=1, source_target_pairs={{0,7},{1,0},{2,1},{3,2},{4,3},{5,4},{6,5},{7,6},{8,15},{9,8},{10,9... | collective-permute-start | bytes 1769480 | tf_op jit(solution)/shard_map/ppermute | solution.py:25
  188.3 37.9 %collective-permute-start.11 = (bf16[1,1,1,2,2,192,384]{6,5,4,3,2,1,0:T(8,128)(2,1)}, bf16[1,1,1,2,2,192,384]{6,5,4,3,2,1,0:T(8,128)(2,1)}, u32[]{:S(2)}, u32[]{:S(2)}) collective-permute-start(bf16[1,1,1,2,2,192,384]{6,5,4,3,2,1,0:T(8,128)(2,1)} %get-tuple-element.80), channel_id=1, source_target_pairs={{0,6},{1,7},{2,0},{3,1},{4,2},{5,3},{6,4},{7,5},{8,14},{9,15},{10,... | collective-permute-start | bytes 1769480 | tf_op jit(solution)/shard_map/ppermute | solution.py:25
  188.3 49.5 %collective-permute-start.20 = (bf16[1,1,1,2,2,192,384]{6,5,4,3,2,1,0:T(8,128)(2,1)}, bf16[1,1,1,2,2,192,384]{6,5,4,3,2,1,0:T(8,128)(2,1)}, u32[]{:S(2)}, u32[]{:S(2)}) collective-permute-start(bf16[1,1,1,2,2,192,384]{6,5,4,3,2,1,0:T(8,128)(2,1)} %get-tuple-element.83), channel_id=1, source_target_pairs={{0,1},{1,2},{2,3},{3,4},{4,5},{5,6},{6,7},{7,0},{8,9},{9,10},{10,1... | collective-permute-start | bytes 1769480 | tf_op jit(solution)/shard_map/ppermute | solution.py:25
  200.7 59.3 %collective-permute-start.21 = (bf16[1,1,1,2,2,192,384]{6,5,4,3,2,1,0:T(8,128)(2,1)}, bf16[1,1,1,2,2,192,384]{6,5,4,3,2,1,0:T(8,128)(2,1)}, u32[]{:S(2)}, u32[]{:S(2)}) collective-permute-start(bf16[1,1,1,2,2,192,384]{6,5,4,3,2,1,0:T(8,128)(2,1)} %get-tuple-element.83), channel_id=1, source_target_pairs={{0,2},{1,3},{2,4},{3,5},{4,6},{5,7},{6,0},{7,1},{8,10},{9,11},{10,... | collective-permute-start | bytes 1769480 | tf_op jit(solution)/shard_map/ppermute | solution.py:25
  201.6 62.5 %collective-permute-start.22 = (bf16[1,1,1,2,2,192,384]{6,5,4,3,2,1,0:T(8,128)(2,1)}, bf16[1,1,1,2,2,192,384]{6,5,4,3,2,1,0:T(8,128)(2,1)}, u32[]{:S(2)}, u32[]{:S(2)}) collective-permute-start(bf16[1,1,1,2,2,192,384]{6,5,4,3,2,1,0:T(8,128)(2,1)} %get-tuple-element.83), channel_id=1, source_target_pairs={{0,7},{1,0},{2,1},{3,2},{4,3},{5,4},{6,5},{7,6},{8,15},{9,8},{10,9... | collective-permute-start | bytes 1769480 | tf_op jit(solution)/shard_map/ppermute | solution.py:25
  226.2 37.9 %collective-permute-start.23 = (bf16[1,1,1,2,2,192,384]{6,5,4,3,2,1,0:T(8,128)(2,1)}, bf16[1,1,1,2,2,192,384]{6,5,4,3,2,1,0:T(8,128)(2,1)}, u32[]{:S(2)}, u32[]{:S(2)}) collective-permute-start(bf16[1,1,1,2,2,192,384]{6,5,4,3,2,1,0:T(8,128)(2,1)} %get-tuple-element.83), channel_id=1, source_target_pairs={{0,6},{1,7},{2,0},{3,1},{4,2},{5,3},{6,4},{7,5},{8,14},{9,15},{10,... | collective-permute-start | bytes 1769480 | tf_op jit(solution)/shard_map/ppermute | solution.py:25
  226.2 49.6 %collective-permute-start.16 = (bf16[1,1,1,2,2,192,384]{6,5,4,3,2,1,0:T(8,128)(2,1)}, bf16[1,1,1,2,2,192,384]{6,5,4,3,2,1,0:T(8,128)(2,1)}, u32[]{:S(2)}, u32[]{:S(2)}) collective-permute-start(bf16[1,1,1,2,2,192,384]{6,5,4,3,2,1,0:T(8,128)(2,1)} %get-tuple-element.79), channel_id=1, source_target_pairs={{0,1},{1,2},{2,3},{3,4},{4,5},{5,6},{6,7},{7,0},{8,9},{9,10},{10,1... | collective-permute-start | bytes 1769480 | tf_op jit(solution)/shard_map/ppermute | solution.py:25
  237.8 38.9 %collective-permute-start.17 = (bf16[1,1,1,2,2,192,384]{6,5,4,3,2,1,0:T(8,128)(2,1)}, bf16[1,1,1,2,2,192,384]{6,5,4,3,2,1,0:T(8,128)(2,1)}, u32[]{:S(2)}, u32[]{:S(2)}) collective-permute-start(bf16[1,1,1,2,2,192,384]{6,5,4,3,2,1,0:T(8,128)(2,1)} %get-tuple-element.79), channel_id=1, source_target_pairs={{0,2},{1,3},{2,4},{3,5},{4,6},{5,7},{6,0},{7,1},{8,10},{9,11},{10,... | collective-permute-start | bytes 1769480 | tf_op jit(solution)/shard_map/ppermute | solution.py:25
  260.1 36.6 %collective-permute-start.18 = (bf16[1,1,1,2,2,192,384]{6,5,4,3,2,1,0:T(8,128)(2,1)}, bf16[1,1,1,2,2,192,384]{6,5,4,3,2,1,0:T(8,128)(2,1)S(1)}, u32[]{:S(2)}, u32[]{:S(2)}) collective-permute-start(bf16[1,1,1,2,2,192,384]{6,5,4,3,2,1,0:T(8,128)(2,1)} %get-tuple-element.79), channel_id=1, source_target_pairs={{0,7},{1,0},{2,1},{3,2},{4,3},{5,4},{6,5},{7,6},{8,15},{9,8},{10,9... | collective-permute-start | bytes 1769480 | tf_op jit(solution)/shard_map/ppermute | solution.py:25
  264.1 37.5 %collective-permute-start.19 = (bf16[1,1,1,2,2,192,384]{6,5,4,3,2,1,0:T(8,128)(2,1)}, bf16[1,1,1,2,2,192,384]{6,5,4,3,2,1,0:T(8,128)(2,1)S(1)}, u32[]{:S(2)}, u32[]{:S(2)}) collective-permute-start(bf16[1,1,1,2,2,192,384]{6,5,4,3,2,1,0:T(8,128)(2,1)} %get-tuple-element.79), channel_id=1, source_target_pairs={{0,6},{1,7},{2,0},{3,1},{4,2},{5,3},{6,4},{7,5},{8,14},{9,15},{10,... | collective-permute-start | bytes 1769480 | tf_op jit(solution)/shard_map/ppermute | solution.py:25
  264.1 49.5 %collective-permute-start.28 = (bf16[1,1,1,2,2,192,384]{6,5,4,3,2,1,0:T(8,128)(2,1)}, bf16[1,1,1,2,2,192,384]{6,5,4,3,2,1,0:T(8,128)(2,1)S(1)}, u32[]{:S(2)}, u32[]{:S(2)}) collective-permute-start(bf16[1,1,1,2,2,192,384]{6,5,4,3,2,1,0:T(8,128)(2,1)} %get-tuple-element.82), channel_id=1, source_target_pairs={{0,1},{1,2},{2,3},{3,4},{4,5},{5,6},{6,7},{7,0},{8,9},{9,10},{10,1... | collective-permute-start | bytes 1769480 | tf_op jit(solution)/shard_map/ppermute | solution.py:25
  275.7 38.8 %collective-permute-start.29 = (bf16[1,1,1,2,2,192,384]{6,5,4,3,2,1,0:T(8,128)(2,1)}, bf16[1,1,1,2,2,192,384]{6,5,4,3,2,1,0:T(8,128)(2,1)S(1)}, u32[]{:S(2)}, u32[]{:S(2)}) collective-permute-start(bf16[1,1,1,2,2,192,384]{6,5,4,3,2,1,0:T(8,128)(2,1)} %get-tuple-element.82), channel_id=1, source_target_pairs={{0,2},{1,3},{2,4},{3,5},{4,6},{5,7},{6,0},{7,1},{8,10},{9,11},{10,... | collective-permute-start | bytes 1769480 | tf_op jit(solution)/shard_map/ppermute | solution.py:25
  276.7 51.6 %collective-permute-start.30 = (bf16[1,1,1,2,2,192,384]{6,5,4,3,2,1,0:T(8,128)(2,1)}, bf16[1,1,1,2,2,192,384]{6,5,4,3,2,1,0:T(8,128)(2,1)S(1)}, u32[]{:S(2)}, u32[]{:S(2)}) collective-permute-start(bf16[1,1,1,2,2,192,384]{6,5,4,3,2,1,0:T(8,128)(2,1)} %get-tuple-element.82), channel_id=1, source_target_pairs={{0,7},{1,0},{2,1},{3,2},{4,3},{5,4},{6,5},{7,6},{8,15},{9,8},{10,9... | collective-permute-start | bytes 1769480 | tf_op jit(solution)/shard_map/ppermute | solution.py:25
  293.6 35.6 %copy-start.31 = (bf16[1,1,1,2,2,192,384]{5,6,4,3,2,1,0:T(8,128)(2,1)S(1)}, bf16[1,1,1,2,2,192,384]{5,6,4,3,2,1,0:T(8,128)(2,1)}, u32[]{:S(2)}) copy-start(bf16[1,1,1,2,2,192,384]{5,6,4,3,2,1,0:T(8,128)(2,1)} %copy.430) | copy-start | bytes 1769476
  293.6 35.6 %copy-start.32 = (bf16[1,1,1,2,2,192,384]{5,6,4,3,2,1,0:T(8,128)(2,1)S(1)}, bf16[1,1,1,2,2,192,384]{5,6,4,3,2,1,0:T(8,128)(2,1)}, u32[]{:S(2)}) copy-start(bf16[1,1,1,2,2,192,384]{5,6,4,3,2,1,0:T(8,128)(2,1)} %copy.431) | copy-start | bytes 1769476
  293.6 35.5 %copy-start.33 = (bf16[1,1,1,2,2,192,384]{5,6,4,3,2,1,0:T(8,128)(2,1)S(1)}, bf16[1,1,1,2,2,192,384]{5,6,4,3,2,1,0:T(8,128)(2,1)}, u32[]{:S(2)}) copy-start(bf16[1,1,1,2,2,192,384]{5,6,4,3,2,1,0:T(8,128)(2,1)} %copy.432) | copy-start | bytes 1769476
  293.6 35.5 %copy-start.34 = (bf16[1,1,1,2,2,192,384]{5,6,4,3,2,1,0:T(8,128)(2,1)S(1)}, bf16[1,1,1,2,2,192,384]{5,6,4,3,2,1,0:T(8,128)(2,1)}, u32[]{:S(2)}) copy-start(bf16[1,1,1,2,2,192,384]{5,6,4,3,2,1,0:T(8,128)(2,1)} %copy.433) | copy-start | bytes 1769476
  296.7 31.6 %copy-start.88 = (bf16[1,1,1,2,2,192,384]{6,5,4,3,2,1,0:T(8,128)(2,1)}, bf16[1,1,1,2,2,192,384]{6,5,4,3,2,1,0:T(8,128)(2,1)S(1)}, u32[]{:S(2)}) copy-start(bf16[1,1,1,2,2,192,384]{6,5,4,3,2,1,0:T(8,128)(2,1)S(1)} %collective-permute-done.18) | copy-start | bytes 1769476
  296.7 68.7 %collective-permute-start.31 = (bf16[1,1,1,2,2,192,384]{6,5,4,3,2,1,0:T(8,128)(2,1)}, bf16[1,1,1,2,2,192,384]{6,5,4,3,2,1,0:T(8,128)(2,1)}, u32[]{:S(2)}, u32[]{:S(2)}) collective-permute-start(bf16[1,1,1,2,2,192,384]{6,5,4,3,2,1,0:T(8,128)(2,1)} %get-tuple-element.82), channel_id=1, source_target_pairs={{0,6},{1,7},{2,0},{3,1},{4,2},{5,3},{6,4},{7,5},{8,14},{9,15},{10,... | collective-permute-start | bytes 1769480 | tf_op jit(solution)/shard_map/ppermute | solution.py:25
  301.6 27.2 %copy-start.90 = (bf16[1,1,1,2,2,192,384]{6,5,4,3,2,1,0:T(8,128)(2,1)}, bf16[1,1,1,2,2,192,384]{6,5,4,3,2,1,0:T(8,128)(2,1)S(1)}, u32[]{:S(2)}) copy-start(bf16[1,1,1,2,2,192,384]{6,5,4,3,2,1,0:T(8,128)(2,1)S(1)} %collective-permute-done.19) | copy-start | bytes 1769476
  301.6 66.0 %collective-permute-start.24 = (bf16[1,1,1,2,2,192,384]{6,5,4,3,2,1,0:T(8,128)(2,1)}, bf16[1,1,1,2,2,192,384]{6,5,4,3,2,1,0:T(8,128)(2,1)}, u32[]{:S(2)}, u32[]{:S(2)}) collective-permute-start(bf16[1,1,1,2,2,192,384]{6,5,4,3,2,1,0:T(8,128)(2,1)} %get-tuple-element.78), channel_id=1, source_target_pairs={{0,1},{1,2},{2,3},{3,4},{4,5},{5,6},{6,7},{7,0},{8,9},{9,10},{10,1... | collective-permute-start | bytes 1769480 | tf_op jit(solution)/shard_map/ppermute | solution.py:25
  313.6 56.2 %collective-permute-start.25 = (bf16[1,1,1,2,2,192,384]{6,5,4,3,2,1,0:T(8,128)(2,1)}, bf16[1,1,1,2,2,192,384]{6,5,4,3,2,1,0:T(8,128)(2,1)}, u32[]{:S(2)}, u32[]{:S(2)}) collective-permute-start(bf16[1,1,1,2,2,192,384]{6,5,4,3,2,1,0:T(8,128)(2,1)} %get-tuple-element.78), channel_id=1, source_target_pairs={{0,2},{1,3},{2,4},{3,5},{4,6},{5,7},{6,0},{7,1},{8,10},{9,11},{10,... | collective-permute-start | bytes 1769480 | tf_op jit(solution)/shard_map/ppermute | solution.py:25
  314.6 57.5 %collective-permute-start.26 = (bf16[1,1,1,2,2,192,384]{6,5,4,3,2,1,0:T(8,128)(2,1)}, bf16[1,1,1,2,2,192,384]{6,5,4,3,2,1,0:T(8,128)(2,1)}, u32[]{:S(2)}, u32[]{:S(2)}) collective-permute-start(bf16[1,1,1,2,2,192,384]{6,5,4,3,2,1,0:T(8,128)(2,1)} %get-tuple-element.78), channel_id=1, source_target_pairs={{0,7},{1,0},{2,1},{3,2},{4,3},{5,4},{6,5},{7,6},{8,15},{9,8},{10,9... | collective-permute-start | bytes 1769480 | tf_op jit(solution)/shard_map/ppermute | solution.py:25
  328.3 48.6 %collective-permute-start.27 = (bf16[1,1,1,2,2,192,384]{6,5,4,3,2,1,0:T(8,128)(2,1)}, bf16[1,1,1,2,2,192,384]{6,5,4,3,2,1,0:T(8,128)(2,1)}, u32[]{:S(2)}, u32[]{:S(2)}) collective-permute-start(bf16[1,1,1,2,2,192,384]{6,5,4,3,2,1,0:T(8,128)(2,1)} %get-tuple-element.78), channel_id=1, source_target_pairs={{0,6},{1,7},{2,0},{3,1},{4,2},{5,3},{6,4},{7,5},{8,14},{9,15},{10,... | collective-permute-start | bytes 1769480 | tf_op jit(solution)/shard_map/ppermute | solution.py:25
  478.1 15.5 %collective-permute-start.32 = (bf16[2,1,1,1,2,384,384]{6,5,4,0,3,2,1:T(8,128)(2,1)}, bf16[2,1,1,1,2,384,384]{6,5,4,0,3,2,1:T(8,128)(2,1)}, u32[]{:S(2)}, u32[]{:S(2)}) collective-permute-start(bf16[2,1,1,1,2,384,384]{6,5,4,0,3,2,1:T(8,128)(2,1)} %bitcast.999), channel_id=1, source_target_pairs={{0,8},{8,0},{16,24},{24,16},{1,9},{9,1},{17,25},{25,17},{2,10},{10... | collective-permute-start | bytes 3538952 | tf_op jit(solution)/shard_map/ppermute | solution.py:214
  479.6 38.6 %collective-permute-start.33 = (bf16[2,1,1,1,2,384,384]{6,5,4,0,3,2,1:T(8,128)(2,1)}, bf16[2,1,1,1,2,384,384]{6,5,4,0,3,2,1:T(8,128)(2,1)S(1)}, u32[]{:S(2)}, u32[]{:S(2)}) collective-permute-start(bf16[2,1,1,1,2,384,384]{6,5,4,0,3,2,1:T(8,128)(2,1)} %bitcast.1000), channel_id=1, source_target_pairs={{0,16},{8,24},{16,0},{24,8},{1,17},{9,25},{17,1},{25,9},{2,18},{10... | collective-permute-start | bytes 3538952 | tf_op jit(solution)/shard_map/ppermute | solution.py:214
  492.6 50.6 %collective-permute-start.34 = (bf16[2,1,1,1,2,384,384]{6,5,4,0,3,2,1:T(8,128)(2,1)}, bf16[2,1,1,1,2,384,384]{6,5,4,0,3,2,1:T(8,128)(2,1)}, u32[]{:S(2)}, u32[]{:S(2)}) collective-permute-start(bf16[2,1,1,1,2,384,384]{6,5,4,0,3,2,1:T(8,128)(2,1)} %bitcast.1001), channel_id=1, source_target_pairs={{0,24},{8,16},{16,8},{24,0},{1,25},{9,17},{17,9},{25,1},{2,26},{10... | collective-permute-start | bytes 3538952 | tf_op jit(solution)/shard_map/ppermute | solution.py:214
  (94 other events, 287.3 us)
Sparse Core Ops, SparseCore 0:
  19.0 39.4 all-gather.4
  151.2 23.0 all-gather.2
